TPU v7x, 256 devices: a whole 4x4x8 slice. The times are simulated.
256 devices in a mesh: gx: 16 (over y, x_lo, core), gy: 16 (over x_hi, z).
Axes of the slice: x: 4 (x_hi: 2, x_lo: 2; x = x_hi * 2 + x_lo), y: 4, z: 8, core: 2. Of those that a mesh axis runs over, the one named last changes fastest.
Arguments:
- blocks: bfloat16 [16, 16, 128, 128, 128], P('gx', 'gy'), may hold values from -0.1875 to 0.1875
- pattern: int32 [16, 16, 128], P('gx', 'gy'), may hold values from 0 to 255, as said below
- local_src: bfloat16 [16, 16, 2, 32, 2048], P('gx', 'gy'), may hold values from -4 to 4
- owner: int32 [2, 32], replicated, may hold values from 0 to 255
Outputs:
- sweep_out: bfloat16 [16, 16, 2, 32, 2048], P('gx', 'gy')
Inputs may be any that keep to these rules, and one draw needn't show every extreme that they name: `pattern`: the 128 values of one cell are distinct.
All inputs are finite; a program needn't handle non-finite values.
Results may differ from a plain program's by a relative error of at most 0.019.
Values may be sent and summed in bfloat16 or wider, within the bound.
No kernel may reach another device: no remote copies, remote signals or barrier semaphores. Data moves between devices by JAX's collectives and lax.ppermute only.
A program may use at most 64 MiB of HBM per device.

v0:
```python
import jax
import jax.numpy as jnp
from jax import lax
from jax.experimental import pallas as pl
from jax.experimental.pallas import tpu as pltpu
from jax.sharding import PartitionSpec as P

VMEM = pl.BlockSpec(memory_space=pltpu.VMEM)
SMEM = pl.BlockSpec(memory_space=pltpu.SMEM)
PARAMS = pltpu.CompilerParams(vmem_limit_bytes=4 * 2**20)


def assemble_kernel(pat, blk, dense):
    count, order, _ = blk.shape
    nblk = dense.shape[0] // order
    dense[...] = jnp.zeros_like(dense)

    def place(k, _):
        row = pl.multiple_of(pat[k] // nblk * order, order)
        col = pl.multiple_of(pat[k] % nblk * order, order)
        dense[pl.ds(col, order), pl.ds(row, order)] = blk[k].T
        return 0

    lax.fori_loop(0, count, place, 0, unroll=8)


def assemble(pat, blk, width):
    return pl.pallas_call(
        assemble_kernel,
        out_shape=pltpu.VMEM((width, width), blk.dtype),
        in_specs=[SMEM, VMEM],
        out_specs=VMEM,
        compiler_params=PARAMS,
        name="assemble",
    )(pat, blk)


def first_kernel(turn, position, dense, source, left, total):
    @pl.when(position[0] == turn)
    def _():
        def columns(n, _):
            cols = pl.ds(pl.multiple_of(n * chunk, chunk), chunk)
            part = jnp.dot(left[...], dense[:trace, cols], preferred_element_type=jnp.float32)
            total[:, cols] = part + source[:, cols].astype(jnp.float32)
            return 0

        trace = left.shape[1]
        chunk = trace // 1
        lax.fori_loop(0, total.shape[1] // chunk, columns, 0)


def second_kernel(turn, half, position, dense, total, bottom, _, out):
    @pl.when(position[0] == turn)
    def _():
        trace = bottom.shape[1]
        cols = slice(half * trace, (half + 1) * trace)
        part = jnp.dot(bottom[...], dense[trace:, cols], preferred_element_type=jnp.float32)
        out[...] = (total[:, cols] + part).astype(out.dtype)


def first(turn, position, dense, source, left):
    return pl.pallas_call(
        lambda *refs: first_kernel(turn, *refs),
        out_shape=pltpu.VMEM(source.shape, jnp.float32),
        in_specs=[SMEM] + [VMEM] * 3,
        out_specs=VMEM,
        compiler_params=PARAMS,
        name="first",
    )(position, dense, source, left)


def second(turn, half, position, dense, total, bottom, out):
    return pl.pallas_call(
        lambda *refs: second_kernel(turn, half, *refs),
        out_shape=jax.ShapeDtypeStruct(out.shape, out.dtype),
        in_specs=[SMEM] + [VMEM] * 4,
        out_specs=VMEM,
        input_output_aliases={4: 0},
        compiler_params=PARAMS,
        name="right" if half == 0 else "top",
    )(position, dense, total, bottom, out)


def pairs(nx, ny, turn, period, across):
    found = []
    for i in range(nx):
        for j in range(ny):
            over, up = (i + 1, j) if across else (i, j + 1)
            if (i + j) % period == turn % period and over < nx and up < ny:
                found.append((i * ny + j, over * ny + up))
    return found


def body(blocks, pattern, local_src, owner):
    nbatch, nsource, width = local_src.shape[2:]
    rows = nbatch * nsource
    trace = width // 2
    period = 16
    nx, ny = lax.axis_size("gx"), lax.axis_size("gy")
    dense = assemble(pattern[0, 0], blocks[0, 0], width)
    x, y = lax.axis_index("gx"), lax.axis_index("gy")
    mine = (owner == x * ny + y)[:, :, None]
    own = local_src[0, 0]
    source = jnp.where(mine, own, jnp.zeros_like(own)).reshape(rows, width)
    position = (x + y).reshape(1)

    right, top = source[:, :trace], source[:, trace:]
    for turn in range(1, nx + ny - 1):
        left = lax.ppermute(right, ("gx", "gy"), pairs(nx, ny, turn - 1, period, True))
        bottom = lax.ppermute(top, ("gx", "gy"), pairs(nx, ny, turn - 1, period, False))
        total = first(turn, position, dense, source, left)
        right = second(turn, 0, position, dense, total, bottom, right)
        top = second(turn, 1, position, dense, total, bottom, top)
    result = jnp.concatenate([right, top], axis=1)
    return result.reshape(1, 1, nbatch, nsource, width)


def solution(mesh):
    return jax.shard_map(
        body,
        mesh=mesh,
        in_specs=(
            P("gx", "gy", None, None, None),
            P("gx", "gy", None),
            P("gx", "gy", None, None, None),
            P(),
        ),
        out_specs=P("gx", "gy", None, None, None),
        check_vma=False,
    )
```

profile of v0, /device:TPU:254, one launch (start us, length us, event | category | flops | bytes accessed | tf_op | source)
XLA Modules:
  0.0 192.3 jit_solution(459227129585946736)
XLA Ops:
  0.0 0.7 broadcast_compare_fusion
  0.8 1.0 bitcast_select_fusion.refs_2_
  3.2 2.2 %copy-done = bf16[1,1,128,128,128]{4,3,2,1,0:T(8,128)(2,1)S(1)} copy-done((bf16[1,1,128,128,128]{4,3,2,1,0:T(8,128)(2,1)S(1)}, bf16[1,1,128,128,128]{4,3,2,1,0:T(8,128)(2,1)}, u32[]{:S(2)}) %copy-start) | copy-done | bytes 4194328
  6.0 3.2 %assemble.1.refs_1_ = bf16[2048,2048]{1,0:T(8,128)(2,1)S(1)} custom-call(s32[128]{0:T(128)S(1)} %bitcast.7, bf16[128,128,128]{2,1,0:T(8,128)(2,1)S(1)} %bitcast.6), custom_call_target="tpu_custom_call" | custom-call | tf_op jit(solution)/shard_map/assemble/pallas_call | solution.py:28
  9.3 0.7 collective-permute-start.2
  11.5 0.7 collective-permute-start.5
  13.6 0.7 collective-permute-start.8
  14.3 0.7 collective-permute-start.9
  17.9 0.7 collective-permute-start.14
  18.6 0.7 collective-permute-start.15
  20.8 0.7 collective-permute-start.18
  22.9 0.7 collective-permute-start.21
  25.2 1.3 collective-permute-start.24
  26.6 1.3 collective-permute-start.25
  27.9 56.7 %collective-permute-done.24.refs_3_ = bf16[64,1024]{1,0:T(8,128)(2,1)S(1)} collective-permute-done((bf16[64,1024]{1,0:T(8,128)(2,1)S(1)}, bf16[64,1024]{1,0:T(8,128)(2,1)S(1)}, u32[]{:S(2)}, u32[]{:S(2)}) %collective-permute-start.24) | collective-permute-done | bytes 131104 | tf_op jit(solution)/shard_map/ppermute | solution.py:109
  84.6 8.9 %collective-permute-done.25.refs_3_ = bf16[64,1024]{1,0:T(8,128)(2,1)S(1)} collective-permute-done((bf16[64,1024]{1,0:T(8,128)(2,1)S(1)}, bf16[64,1024]{1,0:T(8,128)(2,1)S(1)}, u32[]{:S(2)}, u32[]{:S(2)}) %collective-permute-start.25) | collective-permute-done | bytes 131104 | tf_op jit(solution)/shard_map/ppermute | solution.py:110
  93.5 1.3 collective-permute-start.26
  94.8 0.7 collective-permute-start.27
  97.1 0.7 collective-permute-start.30
  97.8 0.7 collective-permute-start.31
  100.0 0.7 collective-permute-start.34
  102.1 0.7 collective-permute-start.37
  104.3 0.7 collective-permute-start.40
  106.4 0.7 collective-permute-start.43
  108.6 0.7 collective-permute-start.46
  109.3 0.7 collective-permute-start.47
  115.9 1.3 collective-permute-start.56
  117.3 1.3 collective-permute-start.57
  118.6 69.0 %collective-permute-done.56.refs_3_ = bf16[64,1024]{1,0:T(8,128)(2,1)S(1)} collective-permute-done((bf16[64,1024]{1,0:T(8,128)(2,1)S(1)}, bf16[64,1024]{1,0:T(8,128)(2,1)S(1)}, u32[]{:S(2)}, u32[]{:S(2)}) %collective-permute-start.56) | collective-permute-done | bytes 131104 | tf_op jit(solution)/shard_map/ppermute | solution.py:109
  187.5 1.0 first.58.refs_2_
  189.0 1.3 collective-permute-start.58
  191.6 0.7 pad_maximum_fusion
  (188 shorter events, 28.1 us)
Async XLA Ops:
  1.8 7.5 %collective-permute-start = (bf16[64,1024]{1,0:T(8,128)(2,1)S(1)}, bf16[64,1024]{1,0:T(8,128)(2,1)S(1)}, u32[]{:S(2)}, u32[]{:S(2)}) collective-permute-start(bf16[64,1024]{1,0:T(8,128)(2,1)S(1)} %get-tuple-element.6.refs_4_), channel_id=1, source_target_pairs={{0,16},{31,47},{46,62},{61,77},{76,92},{91,107},{106,122},{121,137... | collective-permute-start | bytes 393224 | tf_op jit(solution)/shard_map/ppermute | solution.py:109
  2.5 6.8 %collective-permute-start.1 = (bf16[64,1024]{1,0:T(8,128)(2,1)S(1)}, bf16[64,1024]{1,0:T(8,128)(2,1)S(1)}, u32[]{:S(2)}, u32[]{:S(2)}) collective-permute-start(bf16[64,1024]{1,0:T(8,128)(2,1)S(1)} %get-tuple-element.5.refs_4_), channel_id=1, source_target_pairs={{0,1},{46,47},{61,62},{76,77},{91,92},{106,107},{121,122},{136,137... | collective-permute-start | bytes 393224 | tf_op jit(solution)/shard_map/ppermute | solution.py:110
  9.3 1.4 collective-permute-start.2
  10.8 1.4 collective-permute-start.4
  12.2 1.4 collective-permute-start.6
  13.6 1.4 collective-permute-start.8
  15.1 1.4 collective-permute-start.10
  16.5 1.4 collective-permute-start.12
  17.9 1.4 collective-permute-start.14
  19.4 1.4 collective-permute-start.16
  20.8 1.4 collective-permute-start.18
  22.2 1.4 collective-permute-start.20
  23.6 1.4 collective-permute-start.22
  25.2 59.3 %collective-permute-start.24 = (bf16[64,1024]{1,0:T(8,128)(2,1)S(1)}, bf16[64,1024]{1,0:T(8,128)(2,1)S(1)}, u32[]{:S(2)}, u32[]{:S(2)}) collective-permute-start(bf16[64,1024]{1,0:T(8,128)(2,1)S(1)} %right.41.refs_4_), channel_id=1, source_target_pairs={{12,28},{27,43},{42,58},{57,73},{72,88},{87,103},{102,118},{117,13... | collective-permute-start | bytes 393224 | tf_op jit(solution)/shard_map/ppermute | solution.py:109
  26.6 66.9 %collective-permute-start.25 = (bf16[64,1024]{1,0:T(8,128)(2,1)S(1)}, bf16[64,1024]{1,0:T(8,128)(2,1)S(1)}, u32[]{:S(2)}, u32[]{:S(2)}) collective-permute-start(bf16[64,1024]{1,0:T(8,128)(2,1)S(1)} %top.41.refs_4_), channel_id=1, source_target_pairs={{12,13},{27,28},{42,43},{57,58},{72,73},{87,88},{102,103},{117,118... | collective-permute-start | bytes 393224 | tf_op jit(solution)/shard_map/ppermute | solution.py:110
  93.5 2.3 %collective-permute-start.26 = (bf16[64,1024]{1,0:T(8,128)(2,1)S(1)}, bf16[64,1024]{1,0:T(8,128)(2,1)S(1)}, u32[]{:S(2)}, u32[]{:S(2)}) collective-permute-start(bf16[64,1024]{1,0:T(8,128)(2,1)S(1)} %right.42.refs_4_), channel_id=1, source_target_pairs={{13,29},{28,44},{43,59},{58,74},{73,89},{88,104},{103,119},{118,13... | collective-permute-start | bytes 393224 | tf_op jit(solution)/shard_map/ppermute | solution.py:109
  97.1 1.4 collective-permute-start.30
  98.6 1.4 collective-permute-start.32
  100.0 1.4 collective-permute-start.34
  101.4 1.4 collective-permute-start.36
  102.9 1.4 collective-permute-start.38
  104.3 1.4 collective-permute-start.40
  105.7 1.4 collective-permute-start.42
  107.1 1.4 collective-permute-start.44
  108.6 1.4 collective-permute-start.46
  110.2 1.4 collective-permute-start.48
  111.7 1.4 collective-permute-start.50
  113.1 1.4 collective-permute-start.52
  114.5 1.4 collective-permute-start.54
  115.9 71.6 %collective-permute-start.56 = (bf16[64,1024]{1,0:T(8,128)(2,1)S(1)}, bf16[64,1024]{1,0:T(8,128)(2,1)S(1)}, u32[]{:S(2)}, u32[]{:S(2)}) collective-permute-start(bf16[64,1024]{1,0:T(8,128)(2,1)S(1)} %right.57.refs_4_), channel_id=1, source_target_pairs={{12,28},{27,43},{42,58},{57,73},{72,88},{87,103},{102,118},{117,13... | collective-permute-start | bytes 393224 | tf_op jit(solution)/shard_map/ppermute | solution.py:109
  117.3 71.3 %collective-permute-start.57 = (bf16[64,1024]{1,0:T(8,128)(2,1)S(1)}, bf16[64,1024]{1,0:T(8,128)(2,1)S(1)}, u32[]{:S(2)}, u32[]{:S(2)}) collective-permute-start(bf16[64,1024]{1,0:T(8,128)(2,1)S(1)} %top.57.refs_4_), channel_id=1, source_target_pairs={{12,13},{27,28},{42,43},{57,58},{72,73},{87,88},{102,103},{117,118... | collective-permute-start | bytes 393224 | tf_op jit(solution)/shard_map/ppermute | solution.py:110
  189.0 2.5 %collective-permute-start.58 = (bf16[64,1024]{1,0:T(8,128)(2,1)S(1)}, bf16[64,1024]{1,0:T(8,128)(2,1)S(1)}, u32[]{:S(2)}, u32[]{:S(2)}) collective-permute-start(bf16[64,1024]{1,0:T(8,128)(2,1)S(1)} %right.58.refs_4_), channel_id=1, source_target_pairs={{13,29},{28,44},{43,59},{58,74},{73,89},{88,104},{103,119},{118,13... | collective-permute-start | bytes 393224 | tf_op jit(solution)/shard_map/ppermute | solution.py:109
  (30 other events, 24.0 us)
where the time goes:
time: 195 us; the launch traced here: 192 us
  waiting for transfers between devices  135 us (69%)
  starting transfers between devices  43.9 us (23%)
  Pallas kernels  6.41 us (3%)
  local copies, waits for them, and re-layouts  2.94 us (2%)
  other arithmetic  2.44 us (1%)
    ppermute x30, waiting for transfers between devices, body(): lax.ppermute(right, ('gx', 'gy'), pairs(nx, ny, turn - 1, period, True))  126 us
    ppermute x30, starting transfers between devices, body(): lax.ppermute(right, ('gx', 'gy'), pairs(nx, ny, turn - 1, period, True))  22.5 us
    ppermute x30, starting transfers between devices, body(): lax.ppermute(top, ('gx', 'gy'), pairs(nx, ny, turn - 1, period, False))  21.3 us
    ppermute x30, waiting for transfers between devices, body(): lax.ppermute(top, ('gx', 'gy'), pairs(nx, ny, turn - 1, period, False))  8.97 us
  transfers between devices with their start and end apart: 60, of which 4 were waited for; matrix products, arithmetic and copies ran while one was open for 0% of the time, Pallas kernels for 3%

commit v1 on v0

--- a/solution.py
+++ b/solution.py
@@ -7,32 +7,102 @@
 
 VMEM = pl.BlockSpec(memory_space=pltpu.VMEM)
 SMEM = pl.BlockSpec(memory_space=pltpu.SMEM)
+HBM = pl.BlockSpec(memory_space=pltpu.HBM)
+PIECES = 8
 PARAMS = pltpu.CompilerParams(vmem_limit_bytes=4 * 2**20)
 
 
-def assemble_kernel(pat, blk, dense):
+def assemble_kernel(pattern, blocks, dense, pat, blk, pat_done, blk_done):
     count, order, _ = blk.shape
     nblk = dense.shape[0] // order
+    pieces = blk_done.shape[0]
+    piece = count // pieces
+    pat_copy = pltpu.make_async_copy(pattern, pat, pat_done)
+    pat_copy.start()
+
+    def blk_copy(p):
+        part = pl.ds(p * piece, piece)
+        return pltpu.make_async_copy(blocks.at[part], blk.at[part], blk_done.at[p])
+
+    for p in range(pieces):
+        blk_copy(p).start()
     dense[...] = jnp.zeros_like(dense)
+    pat_copy.wait()
 
-    def place(k, _):
-        row = pl.multiple_of(pat[k] // nblk * order, order)
-        col = pl.multiple_of(pat[k] % nblk * order, order)
-        dense[pl.ds(col, order), pl.ds(row, order)] = blk[k].T
+    def settle(p, _):
+        blk_copy(p).wait()
+
+        def place(n, _):
+            k = p * piece + n
+            row = pl.multiple_of(pat[k] // nblk * order, order)
+            col = pl.multiple_of(pat[k] % nblk * order, order)
+            dense[pl.ds(col, order), pl.ds(row, order)] = blk[k].T
+            return 0
+
+        lax.fori_loop(0, piece, place, 0, unroll=8)
         return 0
 
-    lax.fori_loop(0, count, place, 0, unroll=8)
+    lax.fori_loop(0, pieces, settle, 0)
 
 
 def assemble(pat, blk, width):
     return pl.pallas_call(
         assemble_kernel,
         out_shape=pltpu.VMEM((width, width), blk.dtype),
-        in_specs=[SMEM, VMEM],
+        in_specs=[HBM, HBM],
         out_specs=VMEM,
+        scratch_shapes=[
+            pltpu.SMEM(pat.shape, pat.dtype),
+            pltpu.VMEM(blk.shape, blk.dtype),
+            pltpu.SemaphoreType.DMA,
+            pltpu.SemaphoreType.DMA((PIECES,)),
+        ],
+        compiler_params=pltpu.CompilerParams(vmem_limit_bytes=8 * 2**20),
+        name="assemble",
+    )(pltpu.with_memory_space_constraint(pat, pltpu.HBM), pltpu.with_memory_space_constraint(blk, pltpu.HBM))
+
+
+def source_kernel(cell, owner, local, source, right, top, held, who, local_done, who_done):
+    local_copy = pltpu.make_async_copy(local, held, local_done)
+    who_copy = pltpu.make_async_copy(owner, who, who_done)
+    who_copy.start()
+    local_copy.start()
+    nbatch, nsource, width = held.shape
+    trace = width // 2
+    square = (nsource, nsource)
+    diagonal = lax.broadcasted_iota(jnp.int32, square, 0) == lax.broadcasted_iota(jnp.int32, square, 1)
+    who_copy.wait()
+    mine = []
+    for b in range(nbatch):
+        row = jnp.broadcast_to((who[b : b + 1, :] == cell[0]).astype(jnp.float32), square)
+        mine.append(jnp.max(jnp.where(diagonal, row, 0.0), axis=1, keepdims=True) > 0.0)
+    local_copy.wait()
+    for b in range(nbatch):
+        rows = slice(b * nsource, (b + 1) * nsource)
+        own = jnp.where(mine[b], held[b].astype(jnp.float32), 0.0).astype(source.dtype)
+        source[rows, :] = own
+        right[rows, :] = own[:, :trace]
+        top[rows, :] = own[:, trace:]
+
+
+def sources(cell, owner, local):
+    nbatch, nsource, width = local.shape
+    rows = nbatch * nsource
+    half = jax.ShapeDtypeStruct((rows, width // 2), local.dtype)
+    return pl.pallas_call(
+        source_kernel,
+        out_shape=(jax.ShapeDtypeStruct((rows, width), local.dtype), half, half),
+        in_specs=[SMEM, HBM, HBM],
+        out_specs=(VMEM, VMEM, VMEM),
+        scratch_shapes=[
+            pltpu.VMEM(local.shape, local.dtype),
+            pltpu.VMEM(owner.shape, owner.dtype),
+            pltpu.SemaphoreType.DMA,
+            pltpu.SemaphoreType.DMA,
+        ],
         compiler_params=PARAMS,
-        name="assemble",
-    )(pat, blk)
+        name="sources",
+    )(cell, pltpu.with_memory_space_constraint(owner, pltpu.HBM), pltpu.with_memory_space_constraint(local, pltpu.HBM))
 
 
 def first_kernel(turn, position, dense, source, left, total):
@@ -93,18 +163,14 @@
 
 def body(blocks, pattern, local_src, owner):
     nbatch, nsource, width = local_src.shape[2:]
-    rows = nbatch * nsource
     trace = width // 2
     period = 16
     nx, ny = lax.axis_size("gx"), lax.axis_size("gy")
     dense = assemble(pattern[0, 0], blocks[0, 0], width)
     x, y = lax.axis_index("gx"), lax.axis_index("gy")
-    mine = (owner == x * ny + y)[:, :, None]
-    own = local_src[0, 0]
-    source = jnp.where(mine, own, jnp.zeros_like(own)).reshape(rows, width)
+    source, right, top = sources((x * ny + y).reshape(1), owner, local_src[0, 0])
     position = (x + y).reshape(1)
 
-    right, top = source[:, :trace], source[:, trace:]
     for turn in range(1, nx + ny - 1):
         left = lax.ppermute(right, ("gx", "gy"), pairs(nx, ny, turn - 1, period, True))
         bottom = lax.ppermute(top, ("gx", "gy"), pairs(nx, ny, turn - 1, period, False))

time: 195 us -> 192 us (0.985)
  local copies, waits for them, and re-layouts: 2.94 us -> 0 us
    unnamed x4 -> x0, local copies, waits for them, and re-layouts: 2.84 us -> none
where the time goes in v1:
time: 192 us; the launch traced here: 189 us
  waiting for transfers between devices  135 us (70%)
  starting transfers between devices  43.9 us (23%)
  Pallas kernels  7.5 us (4%)
    ppermute x30, waiting for transfers between devices, body(): lax.ppermute(right, ('gx', 'gy'), pairs(nx, ny, turn - 1, period, True))  128 us
    ppermute x30, starting transfers between devices, body(): lax.ppermute(right, ('gx', 'gy'), pairs(nx, ny, turn - 1, period, True))  22.5 us
    ppermute x30, starting transfers between devices, body(): lax.ppermute(top, ('gx', 'gy'), pairs(nx, ny, turn - 1, period, False))  21.3 us
    ppermute x30, waiting for transfers between devices, body(): lax.ppermute(top, ('gx', 'gy'), pairs(nx, ny, turn - 1, period, False))  7.18 us
  transfers between devices with their start and end apart: 60, of which 4 were waited for; matrix products, arithmetic and copies ran while one was open for 0% of the time, Pallas kernels for 3%

profile of v1, /device:TPU:254, one launch (start us, length us, event | category | flops | bytes accessed | tf_op | source)
XLA Modules:
  0.0 188.7 jit_solution(16463647731222224431)
XLA Ops:
  0.0 1.0 sources.1
  2.4 3.3 %assemble.1.refs_1_ = bf16[2048,2048]{1,0:T(8,128)(2,1)S(1)} custom-call(s32[128]{0:T(128)} %bitcast.8, bf16[128,128,128]{2,1,0:T(8,128)(2,1)} %bitcast.6), custom_call_target="tpu_custom_call" | custom-call | tf_op jit(solution)/shard_map/assemble/pallas_call | solution.py:49
  5.8 0.7 collective-permute-start.2
  7.9 0.7 collective-permute-start.5
  10.0 0.7 collective-permute-start.8
  10.7 0.7 collective-permute-start.9
  14.3 0.7 collective-permute-start.14
  15.0 0.7 collective-permute-start.15
  17.2 0.7 collective-permute-start.18
  19.3 0.7 collective-permute-start.21
  21.7 1.3 collective-permute-start.24
  23.0 1.3 collective-permute-start.25
  24.3 58.5 %collective-permute-done.24.refs_3_ = bf16[64,1024]{1,0:T(8,128)(2,1)S(1)} collective-permute-done((bf16[64,1024]{1,0:T(8,128)(2,1)S(1)}, bf16[64,1024]{1,0:T(8,128)(2,1)S(1)}, u32[]{:S(2)}, u32[]{:S(2)}) %collective-permute-start.24) | collective-permute-done | bytes 131104 | tf_op jit(solution)/shard_map/ppermute | solution.py:175
  82.8 7.1 %collective-permute-done.25.refs_3_ = bf16[64,1024]{1,0:T(8,128)(2,1)S(1)} collective-permute-done((bf16[64,1024]{1,0:T(8,128)(2,1)S(1)}, bf16[64,1024]{1,0:T(8,128)(2,1)S(1)}, u32[]{:S(2)}, u32[]{:S(2)}) %collective-permute-start.25) | collective-permute-done | bytes 131104 | tf_op jit(solution)/shard_map/ppermute | solution.py:176
  89.9 1.3 collective-permute-start.26
  91.2 0.7 collective-permute-start.27
  94.3 0.7 collective-permute-start.31
  96.4 0.7 collective-permute-start.34
  97.1 0.7 collective-permute-start.35
  100.7 0.7 collective-permute-start.40
  101.4 0.7 collective-permute-start.41
  103.6 0.7 collective-permute-start.44
  105.7 0.7 collective-permute-start.47
  106.6 0.7 collective-permute-start.48
  108.8 0.7 collective-permute-start.51
  110.9 0.7 collective-permute-start.54
  112.4 1.3 collective-permute-start.56
  113.7 1.3 collective-permute-start.57
  115.0 69.0 %collective-permute-done.56.refs_3_ = bf16[64,1024]{1,0:T(8,128)(2,1)S(1)} collective-permute-done((bf16[64,1024]{1,0:T(8,128)(2,1)S(1)}, bf16[64,1024]{1,0:T(8,128)(2,1)S(1)}, u32[]{:S(2)}, u32[]{:S(2)}) %collective-permute-start.56) | collective-permute-done | bytes 131104 | tf_op jit(solution)/shard_map/ppermute | solution.py:175
  183.9 1.0 first.58.refs_2_
  185.4 1.3 collective-permute-start.58
  188.0 0.7 pad_maximum_fusion
  (181 shorter events, 26.0 us)
Async XLA Ops:
  1.0 4.7 %collective-permute-start = (bf16[64,1024]{1,0:T(8,128)(2,1)S(1)}, bf16[64,1024]{1,0:T(8,128)(2,1)S(1)}, u32[]{:S(2)}, u32[]{:S(2)}) collective-permute-start(bf16[64,1024]{1,0:T(8,128)(2,1)S(1)} %get-tuple-element.9.refs_4_), channel_id=1, source_target_pairs={{0,16},{31,47},{46,62},{61,77},{76,92},{91,107},{106,122},{121,137... | collective-permute-start | bytes 393224 | tf_op jit(solution)/shard_map/ppermute | solution.py:175
  1.7 4.0 %collective-permute-start.1 = (bf16[64,1024]{1,0:T(8,128)(2,1)S(1)}, bf16[64,1024]{1,0:T(8,128)(2,1)S(1)}, u32[]{:S(2)}, u32[]{:S(2)}) collective-permute-start(bf16[64,1024]{1,0:T(8,128)(2,1)S(1)} %get-tuple-element.10.refs_4_), channel_id=1, source_target_pairs={{0,1},{46,47},{61,62},{76,77},{91,92},{106,107},{121,122},{136,137... | collective-permute-start | bytes 393224 | tf_op jit(solution)/shard_map/ppermute | solution.py:176
  5.8 1.4 collective-permute-start.2
  7.2 1.4 collective-permute-start.4
  8.6 1.4 collective-permute-start.6
  10.0 1.4 collective-permute-start.8
  11.5 1.4 collective-permute-start.10
  12.9 1.4 collective-permute-start.12
  14.3 1.4 collective-permute-start.14
  15.8 1.4 collective-permute-start.16
  17.2 1.4 collective-permute-start.18
  18.6 1.4 collective-permute-start.20
  20.0 1.4 collective-permute-start.22
  21.7 61.1 %collective-permute-start.24 = (bf16[64,1024]{1,0:T(8,128)(2,1)S(1)}, bf16[64,1024]{1,0:T(8,128)(2,1)S(1)}, u32[]{:S(2)}, u32[]{:S(2)}) collective-permute-start(bf16[64,1024]{1,0:T(8,128)(2,1)S(1)} %right.41.refs_4_), channel_id=1, source_target_pairs={{12,28},{27,43},{42,58},{57,73},{72,88},{87,103},{102,118},{117,13... | collective-permute-start | bytes 393224 | tf_op jit(solution)/shard_map/ppermute | solution.py:175
  23.0 66.9 %collective-permute-start.25 = (bf16[64,1024]{1,0:T(8,128)(2,1)S(1)}, bf16[64,1024]{1,0:T(8,128)(2,1)S(1)}, u32[]{:S(2)}, u32[]{:S(2)}) collective-permute-start(bf16[64,1024]{1,0:T(8,128)(2,1)S(1)} %top.41.refs_4_), channel_id=1, source_target_pairs={{12,13},{27,28},{42,43},{57,58},{72,73},{87,88},{102,103},{117,118... | collective-permute-start | bytes 393224 | tf_op jit(solution)/shard_map/ppermute | solution.py:176
  89.9 2.3 %collective-permute-start.26 = (bf16[64,1024]{1,0:T(8,128)(2,1)S(1)}, bf16[64,1024]{1,0:T(8,128)(2,1)S(1)}, u32[]{:S(2)}, u32[]{:S(2)}) collective-permute-start(bf16[64,1024]{1,0:T(8,128)(2,1)S(1)} %right.42.refs_4_), channel_id=1, source_target_pairs={{13,29},{28,44},{43,59},{58,74},{73,89},{88,104},{103,119},{118,13... | collective-permute-start | bytes 393224 | tf_op jit(solution)/shard_map/ppermute | solution.py:175
  93.6 1.4 collective-permute-start.30
  95.0 1.4 collective-permute-start.32
  96.4 1.4 collective-permute-start.34
  97.8 1.4 collective-permute-start.36
  99.3 1.4 collective-permute-start.38
  100.7 1.4 collective-permute-start.40
  102.1 1.4 collective-permute-start.42
  103.6 1.4 collective-permute-start.44
  105.0 1.4 collective-permute-start.46
  106.6 1.4 collective-permute-start.48
  108.1 1.4 collective-permute-start.50
  109.5 1.4 collective-permute-start.52
  110.9 1.4 collective-permute-start.54
  112.4 71.6 %collective-permute-start.56 = (bf16[64,1024]{1,0:T(8,128)(2,1)S(1)}, bf16[64,1024]{1,0:T(8,128)(2,1)S(1)}, u32[]{:S(2)}, u32[]{:S(2)}) collective-permute-start(bf16[64,1024]{1,0:T(8,128)(2,1)S(1)} %right.57.refs_4_), channel_id=1, source_target_pairs={{12,28},{27,43},{42,58},{57,73},{72,88},{87,103},{102,118},{117,13... | collective-permute-start | bytes 393224 | tf_op jit(solution)/shard_map/ppermute | solution.py:175
  113.7 71.3 %collective-permute-start.57 = (bf16[64,1024]{1,0:T(8,128)(2,1)S(1)}, bf16[64,1024]{1,0:T(8,128)(2,1)S(1)}, u32[]{:S(2)}, u32[]{:S(2)}) collective-permute-start(bf16[64,1024]{1,0:T(8,128)(2,1)S(1)} %top.57.refs_4_), channel_id=1, source_target_pairs={{12,13},{27,28},{42,43},{57,58},{72,73},{87,88},{102,103},{117,118... | collective-permute-start | bytes 393224 | tf_op jit(solution)/shard_map/ppermute | solution.py:176
  185.4 2.5 %collective-permute-start.58 = (bf16[64,1024]{1,0:T(8,128)(2,1)S(1)}, bf16[64,1024]{1,0:T(8,128)(2,1)S(1)}, u32[]{:S(2)}, u32[]{:S(2)}) collective-permute-start(bf16[64,1024]{1,0:T(8,128)(2,1)S(1)} %right.58.refs_4_), channel_id=1, source_target_pairs={{13,29},{28,44},{43,59},{58,74},{73,89},{88,104},{103,119},{118,13... | collective-permute-start | bytes 393224 | tf_op jit(solution)/shard_map/ppermute | solution.py:175
  (28 other events, 21.1 us)

commit v2 on v1

--- a/solution.py
+++ b/solution.py
@@ -105,30 +105,30 @@
     )(cell, pltpu.with_memory_space_constraint(owner, pltpu.HBM), pltpu.with_memory_space_constraint(local, pltpu.HBM))
 
 
-def first_kernel(turn, position, dense, source, left, total):
+def first_kernel(turn, position, dense, source, bottom, total):
     @pl.when(position[0] == turn)
     def _():
         def columns(n, _):
             cols = pl.ds(pl.multiple_of(n * chunk, chunk), chunk)
-            part = jnp.dot(left[...], dense[:trace, cols], preferred_element_type=jnp.float32)
+            part = jnp.dot(bottom[...], dense[trace:, cols], preferred_element_type=jnp.float32)
             total[:, cols] = part + source[:, cols].astype(jnp.float32)
             return 0
 
-        trace = left.shape[1]
+        trace = bottom.shape[1]
         chunk = trace // 1
         lax.fori_loop(0, total.shape[1] // chunk, columns, 0)
 
 
-def second_kernel(turn, half, position, dense, total, bottom, _, out):
+def second_kernel(turn, half, position, dense, total, left, _, out):
     @pl.when(position[0] == turn)
     def _():
-        trace = bottom.shape[1]
+        trace = left.shape[1]
         cols = slice(half * trace, (half + 1) * trace)
-        part = jnp.dot(bottom[...], dense[trace:, cols], preferred_element_type=jnp.float32)
+        part = jnp.dot(left[...], dense[:trace, cols], preferred_element_type=jnp.float32)
         out[...] = (total[:, cols] + part).astype(out.dtype)
 
 
-def first(turn, position, dense, source, left):
+def first(turn, position, dense, source, bottom):
     return pl.pallas_call(
         lambda *refs: first_kernel(turn, *refs),
         out_shape=pltpu.VMEM(source.shape, jnp.float32),
@@ -136,10 +136,10 @@
         out_specs=VMEM,
         compiler_params=PARAMS,
         name="first",
-    )(position, dense, source, left)
+    )(position, dense, source, bottom)
 
 
-def second(turn, half, position, dense, total, bottom, out):
+def second(turn, half, position, dense, total, left, out):
     return pl.pallas_call(
         lambda *refs: second_kernel(turn, half, *refs),
         out_shape=jax.ShapeDtypeStruct(out.shape, out.dtype),
@@ -148,7 +148,7 @@
         input_output_aliases={4: 0},
         compiler_params=PARAMS,
         name="right" if half == 0 else "top",
-    )(position, dense, total, bottom, out)
+    )(position, dense, total, left, out)
 
 
 def pairs(nx, ny, turn, period, across):
@@ -172,11 +172,11 @@
     position = (x + y).reshape(1)
 
     for turn in range(1, nx + ny - 1):
+        bottom = lax.ppermute(top, ("gx", "gy"), pairs(nx, ny, turn - 1, period, False))
         left = lax.ppermute(right, ("gx", "gy"), pairs(nx, ny, turn - 1, period, True))
-        bottom = lax.ppermute(top, ("gx", "gy"), pairs(nx, ny, turn - 1, period, False))
-        total = first(turn, position, dense, source, left)
-        right = second(turn, 0, position, dense, total, bottom, right)
-        top = second(turn, 1, position, dense, total, bottom, top)
+        total = first(turn, position, dense, source, bottom)
+        top = second(turn, 1, position, dense, total, left, top)
+        right = second(turn, 0, position, dense, total, left, right)
     result = jnp.concatenate([right, top], axis=1)
     return result.reshape(1, 1, nbatch, nsource, width)
 

time: 192 us -> 191 us (level)
    ppermute x30, waiting for transfers between devices: 128 us -> 1.94 us  [body(): lax.ppermute(right, ('gx', 'gy'), pairs(nx, ny, turn - 1, period, True))]
    ppermute x30, waiting for transfers between devices: 7.18 us -> 133 us  [body(): lax.ppermute(top, ('gx', 'gy'), pairs(nx, ny, turn - 1, period, False))]
where the time goes in v2:
time: 191 us; the launch traced here: 188 us
  waiting for transfers between devices  135 us (71%)
  starting transfers between devices  43.9 us (23%)
  Pallas kernels  7.49 us (4%)
    ppermute x30, waiting for transfers between devices, body(): lax.ppermute(top, ('gx', 'gy'), pairs(nx, ny, turn - 1, period, False))  133 us
    ppermute x30, starting transfers between devices, body(): lax.ppermute(right, ('gx', 'gy'), pairs(nx, ny, turn - 1, period, True))  22.6 us
    ppermute x30, starting transfers between devices, body(): lax.ppermute(top, ('gx', 'gy'), pairs(nx, ny, turn - 1, period, False))  21.3 us
  transfers between devices with their start and end apart: 60, of which 4 were waited for; matrix products, arithmetic and copies ran while one was open for 0% of the time, Pallas kernels for 3%

profile of v2, /device:TPU:254, one launch (start us, length us, event | category | flops | bytes accessed | tf_op | source)
XLA Modules:
  0.0 188.5 jit_solution(18110411202454349261)
XLA Ops:
  0.0 1.0 sources.1
  2.4 3.3 %assemble.1.refs_1_ = bf16[2048,2048]{1,0:T(8,128)(2,1)S(1)} custom-call(s32[128]{0:T(128)} %bitcast.8, bf16[128,128,128]{2,1,0:T(8,128)(2,1)} %bitcast.6), custom_call_target="tpu_custom_call" | custom-call | tf_op jit(solution)/shard_map/assemble/pallas_call | solution.py:49
  6.5 0.7 collective-permute-start.3
  8.6 0.7 collective-permute-start.6
  9.3 0.7 collective-permute-start.7
  12.9 0.7 collective-permute-start.12
  13.6 0.7 collective-permute-start.13
  15.8 0.7 collective-permute-start.16
  17.9 0.7 collective-permute-start.19
  20.0 0.7 collective-permute-start.22
  21.7 1.3 collective-permute-start.24
  23.0 1.3 collective-permute-start.25
  24.3 49.3 %collective-permute-done.24.refs_3_ = bf16[64,1024]{1,0:T(8,128)(2,1)S(1)} collective-permute-done((bf16[64,1024]{1,0:T(8,128)(2,1)S(1)}, bf16[64,1024]{1,0:T(8,128)(2,1)S(1)}, u32[]{:S(2)}, u32[]{:S(2)}) %collective-permute-start.24) | collective-permute-done | bytes 131104 | tf_op jit(solution)/shard_map/ppermute | solution.py:175
  74.3 1.3 collective-permute-start.27
  75.6 0.9 collective-permute-done.27.refs_3_
  77.2 0.7 collective-permute-start.29
  80.8 0.7 collective-permute-start.34
  81.5 0.7 collective-permute-start.35
  83.7 0.7 collective-permute-start.38
  85.8 0.7 collective-permute-start.41
  88.0 0.7 collective-permute-start.44
  88.7 0.7 collective-permute-start.45
  91.0 0.7 collective-permute-start.48
  91.7 0.7 collective-permute-start.49
  95.3 0.7 collective-permute-start.54
  96.8 1.3 collective-permute-start.56
  98.1 1.3 collective-permute-start.57
  99.4 83.5 %collective-permute-done.56.refs_3_ = bf16[64,1024]{1,0:T(8,128)(2,1)S(1)} collective-permute-done((bf16[64,1024]{1,0:T(8,128)(2,1)S(1)}, bf16[64,1024]{1,0:T(8,128)(2,1)S(1)}, u32[]{:S(2)}, u32[]{:S(2)}) %collective-permute-start.56) | collective-permute-done | bytes 131104 | tf_op jit(solution)/shard_map/ppermute | solution.py:175
  182.8 1.0 first.58.refs_2_
  185.5 1.3 collective-permute-start.59
  186.8 0.9 collective-permute-done.59.refs_3_
  187.8 0.7 pad_maximum_fusion
  (181 shorter events, 26.4 us)
Async XLA Ops:
  1.0 4.7 %collective-permute-start = (bf16[64,1024]{1,0:T(8,128)(2,1)S(1)}, bf16[64,1024]{1,0:T(8,128)(2,1)S(1)}, u32[]{:S(2)}, u32[]{:S(2)}) collective-permute-start(bf16[64,1024]{1,0:T(8,128)(2,1)S(1)} %get-tuple-element.9.refs_4_), channel_id=1, source_target_pairs={{0,1},{46,47},{61,62},{76,77},{91,92},{106,107},{121,122},{136,137... | collective-permute-start | bytes 393224 | tf_op jit(solution)/shard_map/ppermute | solution.py:175
  1.7 4.0 %collective-permute-start.1 = (bf16[64,1024]{1,0:T(8,128)(2,1)S(1)}, bf16[64,1024]{1,0:T(8,128)(2,1)S(1)}, u32[]{:S(2)}, u32[]{:S(2)}) collective-permute-start(bf16[64,1024]{1,0:T(8,128)(2,1)S(1)} %get-tuple-element.10.refs_4_), channel_id=1, source_target_pairs={{0,16},{31,47},{46,62},{61,77},{76,92},{91,107},{106,122},{121,137... | collective-permute-start | bytes 393224 | tf_op jit(solution)/shard_map/ppermute | solution.py:176
  5.8 1.4 collective-permute-start.2
  7.2 1.4 collective-permute-start.4
  8.6 1.4 collective-permute-start.6
  10.0 1.4 collective-permute-start.8
  11.5 1.4 collective-permute-start.10
  12.9 1.4 collective-permute-start.12
  14.3 1.4 collective-permute-start.14
  15.8 1.4 collective-permute-start.16
  17.2 1.4 collective-permute-start.18
  18.6 1.4 collective-permute-start.20
  20.0 1.4 collective-permute-start.22
  21.7 51.9 %collective-permute-start.24 = (bf16[64,1024]{1,0:T(8,128)(2,1)S(1)}, bf16[64,1024]{1,0:T(8,128)(2,1)S(1)}, u32[]{:S(2)}, u32[]{:S(2)}) collective-permute-start(bf16[64,1024]{1,0:T(8,128)(2,1)S(1)} %top.41.refs_4_), channel_id=1, source_target_pairs={{12,13},{27,28},{42,43},{57,58},{72,73},{87,88},{102,103},{117,118... | collective-permute-start | bytes 393224 | tf_op jit(solution)/shard_map/ppermute | solution.py:175
  23.0 50.6 %collective-permute-start.25 = (bf16[64,1024]{1,0:T(8,128)(2,1)S(1)}, bf16[64,1024]{1,0:T(8,128)(2,1)S(1)}, u32[]{:S(2)}, u32[]{:S(2)}) collective-permute-start(bf16[64,1024]{1,0:T(8,128)(2,1)S(1)} %right.41.refs_4_), channel_id=1, source_target_pairs={{12,28},{27,43},{42,58},{57,73},{72,88},{87,103},{102,118},{117,13... | collective-permute-start | bytes 393224 | tf_op jit(solution)/shard_map/ppermute | solution.py:176
  73.6 2.0 %collective-permute-start.26 = (bf16[64,1024]{1,0:T(8,128)(2,1)S(1)}, bf16[64,1024]{1,0:T(8,128)(2,1)S(1)}, u32[]{:S(2)}, u32[]{:S(2)}) collective-permute-start(bf16[64,1024]{1,0:T(8,128)(2,1)S(1)} %top.42.refs_4_), channel_id=1, source_target_pairs={{13,14},{28,29},{43,44},{58,59},{73,74},{88,89},{103,104},{118,119... | collective-permute-start | bytes 393224 | tf_op jit(solution)/shard_map/ppermute | solution.py:175
  74.3 2.3 %collective-permute-start.27 = (bf16[64,1024]{1,0:T(8,128)(2,1)S(1)}, bf16[64,1024]{1,0:T(8,128)(2,1)S(1)}, u32[]{:S(2)}, u32[]{:S(2)}) collective-permute-start(bf16[64,1024]{1,0:T(8,128)(2,1)S(1)} %right.42.refs_4_), channel_id=1, source_target_pairs={{13,29},{28,44},{43,59},{58,74},{73,89},{88,104},{103,119},{118,13... | collective-permute-start | bytes 393224 | tf_op jit(solution)/shard_map/ppermute | solution.py:176
  78.0 1.4 collective-permute-start.30
  79.4 1.4 collective-permute-start.32
  80.8 1.4 collective-permute-start.34
  82.2 1.4 collective-permute-start.36
  83.7 1.4 collective-permute-start.38
  85.1 1.4 collective-permute-start.40
  86.5 1.4 collective-permute-start.42
  88.0 1.4 collective-permute-start.44
  91.0 1.4 collective-permute-start.48
  93.9 1.4 collective-permute-start.52
  95.3 1.4 collective-permute-start.54
  96.8 86.1 %collective-permute-start.56 = (bf16[64,1024]{1,0:T(8,128)(2,1)S(1)}, bf16[64,1024]{1,0:T(8,128)(2,1)S(1)}, u32[]{:S(2)}, u32[]{:S(2)}) collective-permute-start(bf16[64,1024]{1,0:T(8,128)(2,1)S(1)} %top.57.refs_4_), channel_id=1, source_target_pairs={{12,13},{27,28},{42,43},{57,58},{72,73},{87,88},{102,103},{117,118... | collective-permute-start | bytes 393224 | tf_op jit(solution)/shard_map/ppermute | solution.py:175
  98.1 85.7 %collective-permute-start.57 = (bf16[64,1024]{1,0:T(8,128)(2,1)S(1)}, bf16[64,1024]{1,0:T(8,128)(2,1)S(1)}, u32[]{:S(2)}, u32[]{:S(2)}) collective-permute-start(bf16[64,1024]{1,0:T(8,128)(2,1)S(1)} %right.57.refs_4_), channel_id=1, source_target_pairs={{12,28},{27,43},{42,58},{57,73},{72,88},{87,103},{102,118},{117,13... | collective-permute-start | bytes 393224 | tf_op jit(solution)/shard_map/ppermute | solution.py:176
  184.3 2.5 %collective-permute-start.58 = (bf16[64,1024]{1,0:T(8,128)(2,1)S(1)}, bf16[64,1024]{1,0:T(8,128)(2,1)S(1)}, u32[]{:S(2)}, u32[]{:S(2)}) collective-permute-start(bf16[64,1024]{1,0:T(8,128)(2,1)S(1)} %top.58.refs_4_), channel_id=1, source_target_pairs={{13,14},{28,29},{43,44},{58,59},{73,74},{88,89},{103,104},{118,119... | collective-permute-start | bytes 393224 | tf_op jit(solution)/shard_map/ppermute | solution.py:175
  185.5 2.3 %collective-permute-start.59 = (bf16[64,1024]{1,0:T(8,128)(2,1)S(1)}, bf16[64,1024]{1,0:T(8,128)(2,1)S(1)}, u32[]{:S(2)}, u32[]{:S(2)}) collective-permute-start(bf16[64,1024]{1,0:T(8,128)(2,1)S(1)} %right.58.refs_4_), channel_id=1, source_target_pairs={{13,29},{28,44},{43,59},{58,74},{73,89},{88,104},{103,119},{118,13... | collective-permute-start | bytes 393224 | tf_op jit(solution)/shard_map/ppermute | solution.py:176
  (28 other events, 22.2 us)

commit v3 on v2

--- a/solution.py
+++ b/solution.py
@@ -12,7 +12,7 @@
 PARAMS = pltpu.CompilerParams(vmem_limit_bytes=4 * 2**20)
 
 
-def assemble_kernel(pattern, blocks, dense, pat, blk, pat_done, blk_done):
+def assemble_kernel(_, pattern, blocks, dense, pat, blk, pat_done, blk_done):
     count, order, _ = blk.shape
     nblk = dense.shape[0] // order
     pieces = blk_done.shape[0]
@@ -45,11 +45,11 @@
     lax.fori_loop(0, pieces, settle, 0)
 
 
-def assemble(pat, blk, width):
+def assemble(part, pat, blk, width):
     return pl.pallas_call(
         assemble_kernel,
         out_shape=pltpu.VMEM((width, width), blk.dtype),
-        in_specs=[HBM, HBM],
+        in_specs=[SMEM, HBM, HBM],
         out_specs=VMEM,
         scratch_shapes=[
             pltpu.SMEM(pat.shape, pat.dtype),
@@ -59,7 +59,7 @@
         ],
         compiler_params=pltpu.CompilerParams(vmem_limit_bytes=8 * 2**20),
         name="assemble",
-    )(pltpu.with_memory_space_constraint(pat, pltpu.HBM), pltpu.with_memory_space_constraint(blk, pltpu.HBM))
+    )(part, pltpu.with_memory_space_constraint(pat, pltpu.HBM), pltpu.with_memory_space_constraint(blk, pltpu.HBM))
 
 
 def source_kernel(cell, owner, local, source, right, top, held, who, local_done, who_done):
@@ -105,50 +105,62 @@
     )(cell, pltpu.with_memory_space_constraint(owner, pltpu.HBM), pltpu.with_memory_space_constraint(local, pltpu.HBM))
 
 
-def first_kernel(turn, position, dense, source, bottom, total):
+def touch_kernel(dense, after, out):
+    out[...] = dense[: out.shape[0], : out.shape[1]]
+
+
+def touch(dense, after):
+    return pl.pallas_call(
+        touch_kernel,
+        out_shape=jax.ShapeDtypeStruct((16, 128), dense.dtype),
+        in_specs=[VMEM, pl.BlockSpec(memory_space=pl.ANY)],
+        out_specs=VMEM,
+        compiler_params=PARAMS,
+        name="touch",
+    )(dense, after)
+
+
+def first_kernel(turn, position, dense, source, bottom, *refs):
+    total = refs[-1]
+
     @pl.when(position[0] == turn)
     def _():
-        def columns(n, _):
-            cols = pl.ds(pl.multiple_of(n * chunk, chunk), chunk)
-            part = jnp.dot(bottom[...], dense[trace:, cols], preferred_element_type=jnp.float32)
-            total[:, cols] = part + source[:, cols].astype(jnp.float32)
-            return 0
-
         trace = bottom.shape[1]
-        chunk = trace // 1
-        lax.fori_loop(0, total.shape[1] // chunk, columns, 0)
-
-
-def second_kernel(turn, half, position, dense, total, left, _, out):
+        part = jnp.dot(bottom[...], dense[trace:], preferred_element_type=jnp.float32)
+        total[...] = part + source[...].astype(jnp.float32)
+
+
+def second_kernel(turn, half, position, dense, total, left, swapped, _, out):
     @pl.when(position[0] == turn)
     def _():
         trace = left.shape[1]
         cols = slice(half * trace, (half + 1) * trace)
-        part = jnp.dot(left[...], dense[:trace, cols], preferred_element_type=jnp.float32)
+        given = jnp.where(position[1] == 1, swapped[...], left[...])
+        part = jnp.dot(given, dense[:trace, cols], preferred_element_type=jnp.float32)
         out[...] = (total[:, cols] + part).astype(out.dtype)
 
 
-def first(turn, position, dense, source, bottom):
+def first(turn, position, dense, source, bottom, *after):
     return pl.pallas_call(
         lambda *refs: first_kernel(turn, *refs),
         out_shape=pltpu.VMEM(source.shape, jnp.float32),
-        in_specs=[SMEM] + [VMEM] * 3,
+        in_specs=[SMEM] + [VMEM] * 3 + [pl.BlockSpec(memory_space=pl.ANY)] * len(after),
         out_specs=VMEM,
         compiler_params=PARAMS,
         name="first",
-    )(position, dense, source, bottom)
-
-
-def second(turn, half, position, dense, total, left, out):
+    )(position, dense, source, bottom, *after)
+
+
+def second(turn, half, position, dense, total, left, swapped, out):
     return pl.pallas_call(
         lambda *refs: second_kernel(turn, half, *refs),
         out_shape=jax.ShapeDtypeStruct(out.shape, out.dtype),
-        in_specs=[SMEM] + [VMEM] * 4,
-        out_specs=VMEM,
-        input_output_aliases={4: 0},
+        in_specs=[SMEM] + [VMEM] * 5,
+        out_specs=VMEM,
+        input_output_aliases={5: 0},
         compiler_params=PARAMS,
         name="right" if half == 0 else "top",
-    )(position, dense, total, left, out)
+    )(position, dense, total, left, swapped, out)
 
 
 def pairs(nx, ny, turn, period, across):
@@ -156,7 +168,7 @@
     for i in range(nx):
         for j in range(ny):
             over, up = (i + 1, j) if across else (i, j + 1)
-            if (i + j) % period == turn % period and over < nx and up < ny:
+            if (i + j) % period == turn % period and over < nx and up < ny and not (across and over % 2):
                 found.append((i * ny + j, over * ny + up))
     return found
 
@@ -164,19 +176,28 @@
 def body(blocks, pattern, local_src, owner):
     nbatch, nsource, width = local_src.shape[2:]
     trace = width // 2
-    period = 16
+    period = 15
     nx, ny = lax.axis_size("gx"), lax.axis_size("gy")
-    dense = assemble(pattern[0, 0], blocks[0, 0], width)
     x, y = lax.axis_index("gx"), lax.axis_index("gy")
     source, right, top = sources((x * ny + y).reshape(1), owner, local_src[0, 0])
-    position = (x + y).reshape(1)
-
-    for turn in range(1, nx + ny - 1):
-        bottom = lax.ppermute(top, ("gx", "gy"), pairs(nx, ny, turn - 1, period, False))
-        left = lax.ppermute(right, ("gx", "gy"), pairs(nx, ny, turn - 1, period, True))
-        total = first(turn, position, dense, source, bottom)
-        top = second(turn, 1, position, dense, total, left, top)
-        right = second(turn, 0, position, dense, total, left, right)
+    position = jnp.stack([x + y, x & 1])
+    mates = [(cell, cell ^ ny) for cell in range(nx * ny)]
+
+    def sweep(part, outs):
+        right, top = outs
+        ahead = position - jnp.stack([part * period, 0])
+        dense = assemble(ahead, pattern[0, 0], blocks[0, 0], width)
+        for turn in range(1, period + 1):
+            bottom = lax.ppermute(top, ("gx", "gy"), pairs(nx, ny, turn - 1, period, False))
+            swapped = lax.ppermute(right, ("gx", "gy"), mates)
+            left = lax.ppermute(right, ("gx", "gy"), pairs(nx, ny, turn - 1, period, True))
+            after = [touch(dense, right)] if turn == period else []
+            total = first(turn, ahead, dense, source, bottom, *after)
+            top = second(turn, 1, ahead, dense, total, left, swapped, top)
+            right = second(turn, 0, ahead, dense, total, left, swapped, right)
+        return right, top
+
+    right, top = lax.fori_loop(0, (nx + ny - 2) // period, sweep, (right, top))
     result = jnp.concatenate([right, top], axis=1)
     return result.reshape(1, 1, nbatch, nsource, width)
 

time: 191 us -> 240 us (1.26)
  Pallas kernels: 7.49 us -> 60 us
  waiting for transfers between devices: 135 us -> 109 us
  local copies, waits for them, and re-layouts: 0 us -> 13.5 us
  starting transfers between devices: 43.9 us -> 51.5 us
    pallas_call x60, Pallas kernels: 1.51 us -> 34 us  [second(): pl.pallas_call(lambda *refs: second_kernel(turn, half, *refs), out_shape=...]
    ppermute x60 -> x90, waiting for transfers between devices: 135 us -> 109 us  [the longest x30 108 us: sweep(): lax.ppermute(top, ('gx', 'gy'), pairs(nx, ny, turn - 1, period, False))]
    pallas_call x30, Pallas kernels: 1.66 us -> 17.3 us  [first(): pl.pallas_call(lambda *refs: first_kernel(turn, *refs), out_shape=pltpu.V...]
    while x0 -> x12, local copies, waits for them, and re-layouts: none -> 13.5 us
    ppermute x60 -> x90, starting transfers between devices: 43.9 us -> 51.5 us  [the longest x30 21.3 us: sweep(): lax.ppermute(top, ('gx', 'gy'), pairs(nx, ny, turn - 1, period, False))]
    pallas_call x1 -> x2, Pallas kernels: 3.3 us -> 7.67 us  [assemble(): pl.pallas_call(assemble_kernel, out_shape=pltpu.VMEM((width, width), blk....]
  transfers between devices with their start and end apart: 60 -> 90, of which waited for: 4 -> 3; matrix products, arithmetic and copies ran while one was open for 0% -> 0% of each run, Pallas kernels for 3% -> 17%
where the time goes in v3:
time: 240 us; the launch traced here: 237 us
  waiting for transfers between devices  109 us (45%)
  Pallas kernels  60 us (25%)
  starting transfers between devices  51.5 us (21%)
  local copies, waits for them, and re-layouts  13.5 us (6%)
    ppermute x30, waiting for transfers between devices, sweep(): lax.ppermute(top, ('gx', 'gy'), pairs(nx, ny, turn - 1, period, False))  108 us
    pallas_call x60, Pallas kernels, second(): pl.pallas_call(lambda *refs: second_kernel(turn, half, *refs), out_shape=...  34 us
    ppermute x30, starting transfers between devices, sweep(): lax.ppermute(top, ('gx', 'gy'), pairs(nx, ny, turn - 1, period, False))  21.3 us
    ppermute x30, starting transfers between devices, sweep(): lax.ppermute(right, ('gx', 'gy'), pairs(nx, ny, turn - 1, period, True))  21 us
    pallas_call x30, Pallas kernels, first(): pl.pallas_call(lambda *refs: first_kernel(turn, *refs), out_shape=pltpu.V...  17.3 us
    while x12, local copies, waits for them, and re-layouts  13.5 us
    ppermute x30, starting transfers between devices, sweep(): swapped = lax.ppermute(right, ('gx', 'gy'), mates)  9.22 us
    pallas_call x2, Pallas kernels, assemble(): pl.pallas_call(assemble_kernel, out_shape=pltpu.VMEM((width, width), blk....  7.67 us
  transfers between devices with their start and end apart: 90, of which 3 were waited for; matrix products, arithmetic and copies ran while one was open for 0% of the time, Pallas kernels for 17%

profile of v3, /device:TPU:254, one launch (start us, length us, event | category | flops | bytes accessed | tf_op | source)
XLA Modules:
  0.0 236.7 jit_solution(10697543506565361834)
XLA Ops:
  0.1 1.0 sources.1
  1.1 234.9 %while.15 = (s32[]{:T(128)}, bf16[64,1024]{1,0:T(8,128)(2,1)S(1)}, bf16[64,1024]{1,0:T(8,128)(2,1)S(1)}, s32[2]{0:T(128)S(1)}, s32[1,1,128]{2,1,0:T(1,128)}, /*i...) while((s32[]{:T(128)}, bf16[64,1024]{1,0:T(8,128)(2,1)S(1)}, ...), condition=%wide.region_1.0_spmd, body=%wide.region_0.0_spmd.sunk | while | flops 7 | bytes 124258272 | solution.py:200
  1.1 0.7 collective-permute-start.1
  1.9 0.7 collective-permute-start
  2.7 3.8 %assemble.1.refs_1_.dense = bf16[2048,2048]{1,0:T(8,128)(2,1)S(1)} custom-call(s32[2]{0:T(128)S(1)} %add_subtract_fusion.2._.refs_0_, s32[128]{0:T(128)} %bitcast.16, bf16[128,128,128]{2,1,0:T(8,128)(2,1)} %bitcast.14), custom_call_target="tpu_custom_call" | custom-call | tf_op jit(solution)/shard_map/while/body/eval_jaxpr/assemble/pallas_call | solution.py:49
  7.7 0.7 collective-permute-start.3
  11.3 0.7 collective-permute-start.6
  14.5 0.7 collective-permute-start.9
  34.9 0.7 collective-permute-start.27
  38.4 0.7 collective-permute-start.30
  41.6 0.7 collective-permute-start.33
  45.2 0.7 collective-permute-start.36
  48.4 1.3 collective-permute-start.39
  50.4 1.3 collective-permute-start.40
  51.7 43.9 %collective-permute-done.39.refs_3_ = bf16[64,1024]{1,0:T(8,128)(2,1)S(1)} collective-permute-done((bf16[64,1024]{1,0:T(8,128)(2,1)S(1)}, bf16[64,1024]{1,0:T(8,128)(2,1)S(1)}, u32[]{:S(2)}, u32[]{:S(2)}) %collective-permute-start.39) | collective-permute-done | bytes 131104 | tf_op jit(solution)/shard_map/while/body/eval_jaxpr/ppermute | solution.py:191
  96.7 0.7 collective-permute-start.42
  98.7 3.4 %copy-done.1 = bf16[2048,2048]{1,0:T(8,128)(2,1)S(1)} copy-done((bf16[2048,2048]{1,0:T(8,128)(2,1)S(1)}, bf16[2048,2048]{1,0:T(8,128)(2,1)}, u32[]{:S(2)}) %copy-start.1) | copy-done | bytes 8388632 | tf_op jit(solution)/shard_map/while
  102.1 3.4 %copy-done.2 = bf16[2048,2048]{1,0:T(8,128)(2,1)S(1)} copy-done((bf16[2048,2048]{1,0:T(8,128)(2,1)S(1)}, bf16[2048,2048]{1,0:T(8,128)(2,1)}, u32[]{:S(2)}) %copy-start.2) | copy-done | bytes 8388632 | tf_op jit(solution)/shard_map/while
  107.2 0.7 collective-permute-start.1
  109.2 3.8 %assemble.1.refs_1_.dense = bf16[2048,2048]{1,0:T(8,128)(2,1)S(1)} custom-call(s32[2]{0:T(128)S(1)} %add_subtract_fusion.2._.refs_0_, s32[128]{0:T(128)} %bitcast.16, bf16[128,128,128]{2,1,0:T(8,128)(2,1)} %bitcast.14), custom_call_target="tpu_custom_call" | custom-call | tf_op jit(solution)/shard_map/while/body/eval_jaxpr/assemble/pallas_call | solution.py:49
  114.2 0.7 collective-permute-start.3
  117.4 0.7 collective-permute-start.6
  121.0 0.7 collective-permute-start.9
  154.9 1.3 collective-permute-start.39
  156.8 1.3 collective-permute-start.40
  158.1 64.5 %collective-permute-done.39.refs_3_ = bf16[64,1024]{1,0:T(8,128)(2,1)S(1)} collective-permute-done((bf16[64,1024]{1,0:T(8,128)(2,1)S(1)}, bf16[64,1024]{1,0:T(8,128)(2,1)S(1)}, u32[]{:S(2)}, u32[]{:S(2)}) %collective-permute-start.39) | collective-permute-done | bytes 131104 | tf_op jit(solution)/shard_map/while/body/eval_jaxpr/ppermute | solution.py:191
  222.6 1.4 first.28.refs_2_
  224.0 1.0 top.32.refs_5_
  225.7 1.0 right.32.after.refs_5_
  227.6 3.4 %copy-done.1 = bf16[2048,2048]{1,0:T(8,128)(2,1)S(1)} copy-done((bf16[2048,2048]{1,0:T(8,128)(2,1)S(1)}, bf16[2048,2048]{1,0:T(8,128)(2,1)}, u32[]{:S(2)}) %copy-start.1) | copy-done | bytes 8388632 | tf_op jit(solution)/shard_map/while
  230.9 3.4 %copy-done.2 = bf16[2048,2048]{1,0:T(8,128)(2,1)S(1)} copy-done((bf16[2048,2048]{1,0:T(8,128)(2,1)S(1)}, bf16[2048,2048]{1,0:T(8,128)(2,1)}, u32[]{:S(2)}) %copy-start.2) | copy-done | bytes 8388632 | tf_op jit(solution)/shard_map/while
  236.0 0.7 pad_maximum_fusion
  (260 shorter events, 85.6 us)
Async XLA Ops:
  1.1 6.0 %collective-permute-start.1 = (bf16[64,1024]{1,0:T(8,128)(2,1)S(1)}, bf16[64,1024]{1,0:T(8,128)(2,1)S(1)}, u32[]{:S(2)}, u32[]{:S(2)}) collective-permute-start(bf16[64,1024]{1,0:T(8,128)(2,1)S(1)} %get-tuple-element.198.refs_5_), channel_id=1, source_target_pairs={{30,46},{60,76},{90,106},{120,136},{150,166},{180,196},{210,226}} | collective-permute-start | bytes 393224 | tf_op jit(solution)/shard_map/while/body/eval_jaxpr/ppermute | solution.py:193
  1.8 5.3 %collective-permute-start.2 = (bf16[64,1024]{1,0:T(8,128)(2,1)S(1)}, bf16[64,1024]{1,0:T(8,128)(2,1)S(1)}, u32[]{:S(2)}, u32[]{:S(2)}) collective-permute-start(bf16[64,1024]{1,0:T(8,128)(2,1)S(1)} %get-tuple-element.198.refs_5_), channel_id=1, source_target_pairs={{0,16},{1,17},{2,18},{3,19},{4,20},{5,21},{6,22},{7,23},{8,24},{9,... | collective-permute-start | bytes 393224 | tf_op jit(solution)/shard_map/while/body/eval_jaxpr/ppermute | solution.py:192
  1.9 4.6 %collective-permute-start = (bf16[64,1024]{1,0:T(8,128)(2,1)S(1)}, bf16[64,1024]{1,0:T(8,128)(2,1)S(1)}, u32[]{:S(2)}, u32[]{:S(2)}) collective-permute-start(bf16[64,1024]{1,0:T(8,128)(2,1)S(1)} %get-tuple-element.199.refs_5_), channel_id=1, source_target_pairs={{0,1},{30,31},{45,46},{60,61},{75,76},{90,91},{105,106},{120,121},... | collective-permute-start | bytes 393224 | tf_op jit(solution)/shard_map/while/body/eval_jaxpr/ppermute | solution.py:191
  7.7 2.5 %collective-permute-start.3 = (bf16[64,1024]{1,0:T(8,128)(2,1)S(1)}, bf16[64,1024]{1,0:T(8,128)(2,1)S(1)}, u32[]{:S(2)}, u32[]{:S(2)}) collective-permute-start(bf16[64,1024]{1,0:T(8,128)(2,1)S(1)} %top.19.refs_5_), channel_id=1, source_target_pairs={{1,2},{16,17},{46,47},{61,62},{76,77},{91,92},{106,107},{121,122},... | collective-permute-start | bytes 393224 | tf_op jit(solution)/shard_map/while/body/eval_jaxpr/ppermute | solution.py:191
  14.5 2.4 %collective-permute-start.9 = (bf16[64,1024]{1,0:T(8,128)(2,1)S(1)}, bf16[64,1024]{1,0:T(8,128)(2,1)S(1)}, u32[]{:S(2)}, u32[]{:S(2)}) collective-permute-start(bf16[64,1024]{1,0:T(8,128)(2,1)S(1)} %top.21.refs_5_), channel_id=1, source_target_pairs={{3,4},{18,19},{33,34},{48,49},{78,79},{93,94},{108,109},{123,124},... | collective-permute-start | bytes 393224 | tf_op jit(solution)/shard_map/while/body/eval_jaxpr/ppermute | solution.py:191
  21.3 2.4 %collective-permute-start.15 = (bf16[64,1024]{1,0:T(8,128)(2,1)S(1)}, bf16[64,1024]{1,0:T(8,128)(2,1)S(1)}, u32[]{:S(2)}, u32[]{:S(2)}) collective-permute-start(bf16[64,1024]{1,0:T(8,128)(2,1)S(1)} %top.23.refs_5_), channel_id=1, source_target_pairs={{5,6},{20,21},{35,36},{50,51},{65,66},{80,81},{110,111},{125,126},... | collective-permute-start | bytes 393224 | tf_op jit(solution)/shard_map/while/body/eval_jaxpr/ppermute | solution.py:191
  28.1 2.4 %collective-permute-start.21 = (bf16[64,1024]{1,0:T(8,128)(2,1)S(1)}, bf16[64,1024]{1,0:T(8,128)(2,1)S(1)}, u32[]{:S(2)}, u32[]{:S(2)}) collective-permute-start(bf16[64,1024]{1,0:T(8,128)(2,1)S(1)} %top.25.refs_5_), channel_id=1, source_target_pairs={{7,8},{22,23},{37,38},{52,53},{67,68},{82,83},{97,98},{112,113},{1... | collective-permute-start | bytes 393224 | tf_op jit(solution)/shard_map/while/body/eval_jaxpr/ppermute | solution.py:191
  34.9 2.4 %collective-permute-start.27 = (bf16[64,1024]{1,0:T(8,128)(2,1)S(1)}, bf16[64,1024]{1,0:T(8,128)(2,1)S(1)}, u32[]{:S(2)}, u32[]{:S(2)}) collective-permute-start(bf16[64,1024]{1,0:T(8,128)(2,1)S(1)} %top.27.refs_5_), channel_id=1, source_target_pairs={{9,10},{24,25},{39,40},{54,55},{69,70},{84,85},{99,100},{114,115},... | collective-permute-start | bytes 393224 | tf_op jit(solution)/shard_map/while/body/eval_jaxpr/ppermute | solution.py:191
  38.4 2.1 collective-permute-start.30
  41.6 2.4 %collective-permute-start.33 = (bf16[64,1024]{1,0:T(8,128)(2,1)S(1)}, bf16[64,1024]{1,0:T(8,128)(2,1)S(1)}, u32[]{:S(2)}, u32[]{:S(2)}) collective-permute-start(bf16[64,1024]{1,0:T(8,128)(2,1)S(1)} %top.29.refs_5_), channel_id=1, source_target_pairs={{11,12},{26,27},{41,42},{56,57},{71,72},{86,87},{101,102},{116,117... | collective-permute-start | bytes 393224 | tf_op jit(solution)/shard_map/while/body/eval_jaxpr/ppermute | solution.py:191
  45.2 2.1 collective-permute-start.36
  48.4 47.1 %collective-permute-start.39 = (bf16[64,1024]{1,0:T(8,128)(2,1)S(1)}, bf16[64,1024]{1,0:T(8,128)(2,1)S(1)}, u32[]{:S(2)}, u32[]{:S(2)}) collective-permute-start(bf16[64,1024]{1,0:T(8,128)(2,1)S(1)} %top.31.refs_5_), channel_id=1, source_target_pairs={{13,14},{28,29},{43,44},{58,59},{73,74},{88,89},{103,104},{118,119... | collective-permute-start | bytes 393224 | tf_op jit(solution)/shard_map/while/body/eval_jaxpr/ppermute | solution.py:191
  50.3 45.8 %collective-permute-start.41 = (bf16[64,1024]{1,0:T(8,128)(2,1)S(1)}, bf16[64,1024]{1,0:T(8,128)(2,1)S(1)}, u32[]{:S(2)}, u32[]{:S(2)}) collective-permute-start(bf16[64,1024]{1,0:T(8,128)(2,1)S(1)} %right.31.refs_5_), channel_id=1, source_target_pairs={{0,16},{1,17},{2,18},{3,19},{4,20},{5,21},{6,22},{7,23},{8,24},{9,... | collective-permute-start | bytes 393224 | tf_op jit(solution)/shard_map/while/body/eval_jaxpr/ppermute | solution.py:192
  50.4 45.7 %collective-permute-start.40 = (bf16[64,1024]{1,0:T(8,128)(2,1)S(1)}, bf16[64,1024]{1,0:T(8,128)(2,1)S(1)}, u32[]{:S(2)}, u32[]{:S(2)}) collective-permute-start(bf16[64,1024]{1,0:T(8,128)(2,1)S(1)} %right.31.refs_5_), channel_id=1, source_target_pairs={{28,44},{58,74},{88,104},{118,134},{148,164},{178,194},{208,224},{... | collective-permute-start | bytes 393224 | tf_op jit(solution)/shard_map/while/body/eval_jaxpr/ppermute | solution.py:193
  96.7 5.4 %collective-permute-start.42 = (bf16[64,1024]{1,0:T(8,128)(2,1)S(1)}, bf16[64,1024]{1,0:T(8,128)(2,1)S(1)}, u32[]{:S(2)}, u32[]{:S(2)}) collective-permute-start(bf16[64,1024]{1,0:T(8,128)(2,1)S(1)} %top.32.refs_5_), channel_id=1, source_target_pairs={{14,15},{29,30},{44,45},{59,60},{74,75},{89,90},{104,105},{119,120... | collective-permute-start | bytes 393224 | tf_op jit(solution)/shard_map/while/body/eval_jaxpr/ppermute | solution.py:191
  97.9 8.1 %collective-permute-start.44 = (bf16[64,1024]{1,0:T(8,128)(2,1)S(1)}, bf16[64,1024]{1,0:T(8,128)(2,1)S(1)}, u32[]{:S(2)}, u32[]{:S(2)}) collective-permute-start(bf16[64,1024]{1,0:T(8,128)(2,1)S(1)} %right.32.after.refs_5_), channel_id=1, source_target_pairs={{0,16},{1,17},{2,18},{3,19},{4,20},{5,21},{6,22},{7,23},{8,24},{9,... | collective-permute-start | bytes 393224 | tf_op jit(solution)/shard_map/while/body/eval_jaxpr/ppermute | solution.py:192
  98.0 8.0 %collective-permute-start.43 = (bf16[64,1024]{1,0:T(8,128)(2,1)S(1)}, bf16[64,1024]{1,0:T(8,128)(2,1)S(1)}, u32[]{:S(2)}, u32[]{:S(2)}) collective-permute-start(bf16[64,1024]{1,0:T(8,128)(2,1)S(1)} %right.32.after.refs_5_), channel_id=1, source_target_pairs={{29,45},{59,75},{89,105},{119,135},{149,165},{179,195},{209,225}} | collective-permute-start | bytes 393224 | tf_op jit(solution)/shard_map/while/body/eval_jaxpr/ppermute | solution.py:193
  107.2 6.4 %collective-permute-start.1 = (bf16[64,1024]{1,0:T(8,128)(2,1)S(1)}, bf16[64,1024]{1,0:T(8,128)(2,1)S(1)}, u32[]{:S(2)}, u32[]{:S(2)}) collective-permute-start(bf16[64,1024]{1,0:T(8,128)(2,1)S(1)} %get-tuple-element.198.refs_5_), channel_id=1, source_target_pairs={{30,46},{60,76},{90,106},{120,136},{150,166},{180,196},{210,226}} | collective-permute-start | bytes 393224 | tf_op jit(solution)/shard_map/while/body/eval_jaxpr/ppermute | solution.py:193
  107.9 5.8 %collective-permute-start.2 = (bf16[64,1024]{1,0:T(8,128)(2,1)S(1)}, bf16[64,1024]{1,0:T(8,128)(2,1)S(1)}, u32[]{:S(2)}, u32[]{:S(2)}) collective-permute-start(bf16[64,1024]{1,0:T(8,128)(2,1)S(1)} %get-tuple-element.198.refs_5_), channel_id=1, source_target_pairs={{0,16},{1,17},{2,18},{3,19},{4,20},{5,21},{6,22},{7,23},{8,24},{9,... | collective-permute-start | bytes 393224 | tf_op jit(solution)/shard_map/while/body/eval_jaxpr/ppermute | solution.py:192
  108.4 4.6 %collective-permute-start = (bf16[64,1024]{1,0:T(8,128)(2,1)S(1)}, bf16[64,1024]{1,0:T(8,128)(2,1)S(1)}, u32[]{:S(2)}, u32[]{:S(2)}) collective-permute-start(bf16[64,1024]{1,0:T(8,128)(2,1)S(1)} %get-tuple-element.199.refs_5_), channel_id=1, source_target_pairs={{0,1},{30,31},{45,46},{60,61},{75,76},{90,91},{105,106},{120,121},... | collective-permute-start | bytes 393224 | tf_op jit(solution)/shard_map/while/body/eval_jaxpr/ppermute | solution.py:191
  117.4 2.4 %collective-permute-start.6 = (bf16[64,1024]{1,0:T(8,128)(2,1)S(1)}, bf16[64,1024]{1,0:T(8,128)(2,1)S(1)}, u32[]{:S(2)}, u32[]{:S(2)}) collective-permute-start(bf16[64,1024]{1,0:T(8,128)(2,1)S(1)} %top.20.refs_5_), channel_id=1, source_target_pairs={{2,3},{17,18},{32,33},{62,63},{77,78},{92,93},{107,108},{122,123},... | collective-permute-start | bytes 393224 | tf_op jit(solution)/shard_map/while/body/eval_jaxpr/ppermute | solution.py:191
  124.2 2.4 %collective-permute-start.12 = (bf16[64,1024]{1,0:T(8,128)(2,1)S(1)}, bf16[64,1024]{1,0:T(8,128)(2,1)S(1)}, u32[]{:S(2)}, u32[]{:S(2)}) collective-permute-start(bf16[64,1024]{1,0:T(8,128)(2,1)S(1)} %top.22.refs_5_), channel_id=1, source_target_pairs={{4,5},{19,20},{34,35},{49,50},{64,65},{94,95},{109,110},{124,125},... | collective-permute-start | bytes 393224 | tf_op jit(solution)/shard_map/while/body/eval_jaxpr/ppermute | solution.py:191
  131.0 2.4 %collective-permute-start.18 = (bf16[64,1024]{1,0:T(8,128)(2,1)S(1)}, bf16[64,1024]{1,0:T(8,128)(2,1)S(1)}, u32[]{:S(2)}, u32[]{:S(2)}) collective-permute-start(bf16[64,1024]{1,0:T(8,128)(2,1)S(1)} %top.24.refs_5_), channel_id=1, source_target_pairs={{6,7},{21,22},{36,37},{51,52},{66,67},{81,82},{96,97},{126,127},{1... | collective-permute-start | bytes 393224 | tf_op jit(solution)/shard_map/while/body/eval_jaxpr/ppermute | solution.py:191
  137.7 2.4 %collective-permute-start.24 = (bf16[64,1024]{1,0:T(8,128)(2,1)S(1)}, bf16[64,1024]{1,0:T(8,128)(2,1)S(1)}, u32[]{:S(2)}, u32[]{:S(2)}) collective-permute-start(bf16[64,1024]{1,0:T(8,128)(2,1)S(1)} %top.26.refs_5_), channel_id=1, source_target_pairs={{8,9},{23,24},{38,39},{53,54},{68,69},{83,84},{98,99},{113,114},{1... | collective-permute-start | bytes 393224 | tf_op jit(solution)/shard_map/while/body/eval_jaxpr/ppermute | solution.py:191
  144.5 2.4 %collective-permute-start.30 = (bf16[64,1024]{1,0:T(8,128)(2,1)S(1)}, bf16[64,1024]{1,0:T(8,128)(2,1)S(1)}, u32[]{:S(2)}, u32[]{:S(2)}) collective-permute-start(bf16[64,1024]{1,0:T(8,128)(2,1)S(1)} %top.28.refs_5_), channel_id=1, source_target_pairs={{10,11},{25,26},{40,41},{55,56},{70,71},{85,86},{100,101},{115,116... | collective-permute-start | bytes 393224 | tf_op jit(solution)/shard_map/while/body/eval_jaxpr/ppermute | solution.py:191
  151.3 2.4 %collective-permute-start.36 = (bf16[64,1024]{1,0:T(8,128)(2,1)S(1)}, bf16[64,1024]{1,0:T(8,128)(2,1)S(1)}, u32[]{:S(2)}, u32[]{:S(2)}) collective-permute-start(bf16[64,1024]{1,0:T(8,128)(2,1)S(1)} %top.30.refs_5_), channel_id=1, source_target_pairs={{12,13},{27,28},{42,43},{57,58},{72,73},{87,88},{102,103},{117,118... | collective-permute-start | bytes 393224 | tf_op jit(solution)/shard_map/while/body/eval_jaxpr/ppermute | solution.py:191
  154.9 67.8 %collective-permute-start.39 = (bf16[64,1024]{1,0:T(8,128)(2,1)S(1)}, bf16[64,1024]{1,0:T(8,128)(2,1)S(1)}, u32[]{:S(2)}, u32[]{:S(2)}) collective-permute-start(bf16[64,1024]{1,0:T(8,128)(2,1)S(1)} %top.31.refs_5_), channel_id=1, source_target_pairs={{13,14},{28,29},{43,44},{58,59},{73,74},{88,89},{103,104},{118,119... | collective-permute-start | bytes 393224 | tf_op jit(solution)/shard_map/while/body/eval_jaxpr/ppermute | solution.py:191
  156.7 67.3 %collective-permute-start.41 = (bf16[64,1024]{1,0:T(8,128)(2,1)S(1)}, bf16[64,1024]{1,0:T(8,128)(2,1)S(1)}, u32[]{:S(2)}, u32[]{:S(2)}) collective-permute-start(bf16[64,1024]{1,0:T(8,128)(2,1)S(1)} %right.31.refs_5_), channel_id=1, source_target_pairs={{0,16},{1,17},{2,18},{3,19},{4,20},{5,21},{6,22},{7,23},{8,24},{9,... | collective-permute-start | bytes 393224 | tf_op jit(solution)/shard_map/while/body/eval_jaxpr/ppermute | solution.py:192
  156.8 67.2 %collective-permute-start.40 = (bf16[64,1024]{1,0:T(8,128)(2,1)S(1)}, bf16[64,1024]{1,0:T(8,128)(2,1)S(1)}, u32[]{:S(2)}, u32[]{:S(2)}) collective-permute-start(bf16[64,1024]{1,0:T(8,128)(2,1)S(1)} %right.31.refs_5_), channel_id=1, source_target_pairs={{28,44},{58,74},{88,104},{118,134},{148,164},{178,194},{208,224},{... | collective-permute-start | bytes 393224 | tf_op jit(solution)/shard_map/while/body/eval_jaxpr/ppermute | solution.py:193
  225.1 5.9 %collective-permute-start.42 = (bf16[64,1024]{1,0:T(8,128)(2,1)S(1)}, bf16[64,1024]{1,0:T(8,128)(2,1)S(1)}, u32[]{:S(2)}, u32[]{:S(2)}) collective-permute-start(bf16[64,1024]{1,0:T(8,128)(2,1)S(1)} %top.32.refs_5_), channel_id=1, source_target_pairs={{14,15},{29,30},{44,45},{59,60},{74,75},{89,90},{104,105},{119,120... | collective-permute-start | bytes 393224 | tf_op jit(solution)/shard_map/while/body/eval_jaxpr/ppermute | solution.py:191
  226.8 8.1 %collective-permute-start.44 = (bf16[64,1024]{1,0:T(8,128)(2,1)S(1)}, bf16[64,1024]{1,0:T(8,128)(2,1)S(1)}, u32[]{:S(2)}, u32[]{:S(2)}) collective-permute-start(bf16[64,1024]{1,0:T(8,128)(2,1)S(1)} %right.32.after.refs_5_), channel_id=1, source_target_pairs={{0,16},{1,17},{2,18},{3,19},{4,20},{5,21},{6,22},{7,23},{8,24},{9,... | collective-permute-start | bytes 393224 | tf_op jit(solution)/shard_map/while/body/eval_jaxpr/ppermute | solution.py:192
  226.9 8.0 %collective-permute-start.43 = (bf16[64,1024]{1,0:T(8,128)(2,1)S(1)}, bf16[64,1024]{1,0:T(8,128)(2,1)S(1)}, u32[]{:S(2)}, u32[]{:S(2)}) collective-permute-start(bf16[64,1024]{1,0:T(8,128)(2,1)S(1)} %right.32.after.refs_5_), channel_id=1, source_target_pairs={{29,45},{59,75},{89,105},{119,135},{149,165},{179,195},{209,225}} | collective-permute-start | bytes 393224 | tf_op jit(solution)/shard_map/while/body/eval_jaxpr/ppermute | solution.py:193
  (64 other events, 306.1 us)

commit v4 on v3

--- a/solution.py
+++ b/solution.py
@@ -130,13 +130,12 @@
         total[...] = part + source[...].astype(jnp.float32)
 
 
-def second_kernel(turn, half, position, dense, total, left, swapped, _, out):
+def second_kernel(turn, half, position, dense, total, left, _, out):
     @pl.when(position[0] == turn)
     def _():
         trace = left.shape[1]
         cols = slice(half * trace, (half + 1) * trace)
-        given = jnp.where(position[1] == 1, swapped[...], left[...])
-        part = jnp.dot(given, dense[:trace, cols], preferred_element_type=jnp.float32)
+        part = jnp.dot(left[...], dense[:trace, cols], preferred_element_type=jnp.float32)
         out[...] = (total[:, cols] + part).astype(out.dtype)
 
 
@@ -151,16 +150,16 @@
     )(position, dense, source, bottom, *after)
 
 
-def second(turn, half, position, dense, total, left, swapped, out):
+def second(turn, half, position, dense, total, left, out):
     return pl.pallas_call(
         lambda *refs: second_kernel(turn, half, *refs),
         out_shape=jax.ShapeDtypeStruct(out.shape, out.dtype),
-        in_specs=[SMEM] + [VMEM] * 5,
-        out_specs=VMEM,
-        input_output_aliases={5: 0},
+        in_specs=[SMEM] + [VMEM] * 4,
+        out_specs=VMEM,
+        input_output_aliases={4: 0},
         compiler_params=PARAMS,
         name="right" if half == 0 else "top",
-    )(position, dense, total, left, swapped, out)
+    )(position, dense, total, left, out)
 
 
 def pairs(nx, ny, turn, period, across):
@@ -168,7 +167,7 @@
     for i in range(nx):
         for j in range(ny):
             over, up = (i + 1, j) if across else (i, j + 1)
-            if (i + j) % period == turn % period and over < nx and up < ny and not (across and over % 2):
+            if (i + j) % period == turn % period and over < nx and up < ny:
                 found.append((i * ny + j, over * ny + up))
     return found
 
@@ -180,21 +179,19 @@
     nx, ny = lax.axis_size("gx"), lax.axis_size("gy")
     x, y = lax.axis_index("gx"), lax.axis_index("gy")
     source, right, top = sources((x * ny + y).reshape(1), owner, local_src[0, 0])
-    position = jnp.stack([x + y, x & 1])
-    mates = [(cell, cell ^ ny) for cell in range(nx * ny)]
+    position = (x + y).reshape(1)
 
     def sweep(part, outs):
         right, top = outs
-        ahead = position - jnp.stack([part * period, 0])
+        ahead = position - part * period
         dense = assemble(ahead, pattern[0, 0], blocks[0, 0], width)
         for turn in range(1, period + 1):
             bottom = lax.ppermute(top, ("gx", "gy"), pairs(nx, ny, turn - 1, period, False))
-            swapped = lax.ppermute(right, ("gx", "gy"), mates)
             left = lax.ppermute(right, ("gx", "gy"), pairs(nx, ny, turn - 1, period, True))
             after = [touch(dense, right)] if turn == period else []
             total = first(turn, ahead, dense, source, bottom, *after)
-            top = second(turn, 1, ahead, dense, total, left, swapped, top)
-            right = second(turn, 0, ahead, dense, total, left, swapped, right)
+            top = second(turn, 1, ahead, dense, total, left, top)
+            right = second(turn, 0, ahead, dense, total, left, right)
         return right, top
 
     right, top = lax.fori_loop(0, (nx + ny - 2) // period, sweep, (right, top))

time: 240 us -> 194 us (0.81)
  Pallas kernels: 60 us -> 10.2 us
  waiting for transfers between devices: 109 us -> 123 us
  starting transfers between devices: 51.5 us -> 43.9 us
    pallas_call x60, Pallas kernels: 34 us -> 1.5 us  [second(): pl.pallas_call(lambda *refs: second_kernel(turn, half, *refs), out_shape=...]
    pallas_call x30, Pallas kernels: 17.3 us -> 1.11 us  [first(): pl.pallas_call(lambda *refs: first_kernel(turn, *refs), out_shape=pltpu.V...]
    ppermute x30, waiting for transfers between devices: 108 us -> 123 us  [sweep(): lax.ppermute(top, ('gx', 'gy'), pairs(nx, ny, turn - 1, period, False))]
    ppermute x30 -> x0, starting transfers between devices: 9.22 us -> none  [sweep(): swapped = lax.ppermute(right, ('gx', 'gy'), mates)]
  transfers between devices with their start and end apart: 90 -> 60, of which waited for: 3 -> 2; matrix products, arithmetic and copies ran while one was open for 0% -> 0% of each run, Pallas kernels for 17% -> 4%
where the time goes in v4:
time: 194 us; the launch traced here: 193 us
  waiting for transfers between devices  123 us (63%)
  starting transfers between devices  43.9 us (23%)
  local copies, waits for them, and re-layouts  13.5 us (7%)
  Pallas kernels  10.2 us (5%)
    ppermute x30, waiting for transfers between devices, sweep(): lax.ppermute(top, ('gx', 'gy'), pairs(nx, ny, turn - 1, period, False))  123 us
    ppermute x30, starting transfers between devices, sweep(): lax.ppermute(right, ('gx', 'gy'), pairs(nx, ny, turn - 1, period, True))  22.6 us
    ppermute x30, starting transfers between devices, sweep(): lax.ppermute(top, ('gx', 'gy'), pairs(nx, ny, turn - 1, period, False))  21.3 us
    while x12, local copies, waits for them, and re-layouts  13.5 us
    pallas_call x2, Pallas kernels, assemble(): pl.pallas_call(assemble_kernel, out_shape=pltpu.VMEM((width, width), blk....  6.6 us
  transfers between devices with their start and end apart: 60, of which 2 were waited for; matrix products, arithmetic and copies ran while one was open for 0% of the time, Pallas kernels for 4%

profile of v4, /device:TPU:254, one launch (start us, length us, event | category | flops | bytes accessed | tf_op | source)
XLA Modules:
  0.0 193.0 jit_solution(13151122414181489420)
XLA Ops:
  0.0 1.0 sources.1
  1.0 191.3 %while.15 = (s32[]{:T(128)}, bf16[64,1024]{1,0:T(8,128)(2,1)S(1)}, bf16[64,1024]{1,0:T(8,128)(2,1)S(1)}, s32[1]{0:T(128)}, s32[1,1,128]{2,1,0:T(1,128)}, /*index...) while((s32[]{:T(128)}, bf16[64,1024]{1,0:T(8,128)(2,1)S(1)}, ...), condition=%wide.region_1.0_spmd, body=%wide.region_0.0_spmd.sunk | while | flops 4 | bytes 116393344 | solution.py:197
  2.4 3.3 %assemble.1.refs_1_.dense = bf16[2048,2048]{1,0:T(8,128)(2,1)S(1)} custom-call(s32[1]{0:T(128)S(6)} %sub.11._.refs_0_, s32[128]{0:T(128)} %bitcast.15, bf16[128,128,128]{2,1,0:T(8,128)(2,1)} %bitcast.13), custom_call_target="tpu_custom_call" | custom-call | tf_op jit(solution)/shard_map/while/body/eval_jaxpr/assemble/pallas_call | solution.py:49
  5.8 0.7 collective-permute-start.2
  7.2 0.7 collective-permute-start.4
  8.6 0.7 collective-permute-start.6
  9.3 0.7 collective-permute-start.7
  10.1 0.7 collective-permute-start.8
  10.8 0.7 collective-permute-start.9
  11.5 0.7 collective-permute-start.10
  12.2 0.7 collective-permute-start.11
  12.9 0.7 collective-permute-start.12
  13.6 0.7 collective-permute-start.13
  15.0 0.7 collective-permute-start.15
  16.5 0.7 collective-permute-start.17
  17.9 0.7 collective-permute-start.19
  22.9 1.3 collective-permute-start.26
  24.2 1.3 collective-permute-start.27
  25.5 52.9 %collective-permute-done.26.refs_3_ = bf16[64,1024]{1,0:T(8,128)(2,1)S(1)} collective-permute-done((bf16[64,1024]{1,0:T(8,128)(2,1)S(1)}, bf16[64,1024]{1,0:T(8,128)(2,1)S(1)}, u32[]{:S(2)}, u32[]{:S(2)}) %collective-permute-start.26) | collective-permute-done | bytes 131104 | tf_op jit(solution)/shard_map/while/body/eval_jaxpr/ppermute | solution.py:189
  79.1 1.3 collective-permute-start.29
  80.4 3.4 %copy-done.1 = bf16[2048,2048]{1,0:T(8,128)(2,1)S(1)} copy-done((bf16[2048,2048]{1,0:T(8,128)(2,1)S(1)}, bf16[2048,2048]{1,0:T(8,128)(2,1)}, u32[]{:S(2)}) %copy-start.1) | copy-done | bytes 8388632 | tf_op jit(solution)/shard_map/while
  83.8 3.4 %copy-done.2 = bf16[2048,2048]{1,0:T(8,128)(2,1)S(1)} copy-done((bf16[2048,2048]{1,0:T(8,128)(2,1)S(1)}, bf16[2048,2048]{1,0:T(8,128)(2,1)}, u32[]{:S(2)}) %copy-start.2) | copy-done | bytes 8388632 | tf_op jit(solution)/shard_map/while
  88.5 3.3 %assemble.1.refs_1_.dense = bf16[2048,2048]{1,0:T(8,128)(2,1)S(1)} custom-call(s32[1]{0:T(128)S(6)} %sub.11._.refs_0_, s32[128]{0:T(128)} %bitcast.15, bf16[128,128,128]{2,1,0:T(8,128)(2,1)} %bitcast.13), custom_call_target="tpu_custom_call" | custom-call | tf_op jit(solution)/shard_map/while/body/eval_jaxpr/assemble/pallas_call | solution.py:49
  91.9 0.7 collective-permute-start.2
  109.1 1.3 collective-permute-start.26
  110.4 1.3 collective-permute-start.27
  111.7 70.0 %collective-permute-done.26.refs_3_ = bf16[64,1024]{1,0:T(8,128)(2,1)S(1)} collective-permute-done((bf16[64,1024]{1,0:T(8,128)(2,1)S(1)}, bf16[64,1024]{1,0:T(8,128)(2,1)S(1)}, u32[]{:S(2)}, u32[]{:S(2)}) %collective-permute-start.26) | collective-permute-done | bytes 131104 | tf_op jit(solution)/shard_map/while/body/eval_jaxpr/ppermute | solution.py:189
  181.7 0.8 first.28.refs_2_
  184.2 1.3 collective-permute-start.29
  185.5 3.4 %copy-done.1 = bf16[2048,2048]{1,0:T(8,128)(2,1)S(1)} copy-done((bf16[2048,2048]{1,0:T(8,128)(2,1)S(1)}, bf16[2048,2048]{1,0:T(8,128)(2,1)}, u32[]{:S(2)}) %copy-start.1) | copy-done | bytes 8388632 | tf_op jit(solution)/shard_map/while
  188.9 3.4 %copy-done.2 = bf16[2048,2048]{1,0:T(8,128)(2,1)S(1)} copy-done((bf16[2048,2048]{1,0:T(8,128)(2,1)S(1)}, bf16[2048,2048]{1,0:T(8,128)(2,1)}, u32[]{:S(2)}) %copy-start.2) | copy-done | bytes 8388632 | tf_op jit(solution)/shard_map/while
  192.3 0.7 pad_maximum_fusion
  (197 shorter events, 28.7 us)
Async XLA Ops:
  1.0 4.7 %collective-permute-start = (bf16[64,1024]{1,0:T(8,128)(2,1)S(1)}, bf16[64,1024]{1,0:T(8,128)(2,1)S(1)}, u32[]{:S(2)}, u32[]{:S(2)}) collective-permute-start(bf16[64,1024]{1,0:T(8,128)(2,1)S(1)} %get-tuple-element.198.refs_4_), channel_id=1, source_target_pairs={{0,1},{30,31},{45,46},{60,61},{75,76},{90,91},{105,106},{120,121},... | collective-permute-start | bytes 393224 | tf_op jit(solution)/shard_map/while/body/eval_jaxpr/ppermute | solution.py:189
  1.7 4.0 %collective-permute-start.1 = (bf16[64,1024]{1,0:T(8,128)(2,1)S(1)}, bf16[64,1024]{1,0:T(8,128)(2,1)S(1)}, u32[]{:S(2)}, u32[]{:S(2)}) collective-permute-start(bf16[64,1024]{1,0:T(8,128)(2,1)S(1)} %get-tuple-element.197.refs_4_), channel_id=1, source_target_pairs={{0,16},{15,31},{30,46},{45,61},{60,76},{75,91},{90,106},{105,121},... | collective-permute-start | bytes 393224 | tf_op jit(solution)/shard_map/while/body/eval_jaxpr/ppermute | solution.py:190
  5.8 1.4 collective-permute-start.2
  7.2 1.4 collective-permute-start.4
  8.6 1.4 collective-permute-start.6
  10.1 1.4 collective-permute-start.8
  11.5 1.4 collective-permute-start.10
  12.9 1.4 collective-permute-start.12
  14.4 1.4 collective-permute-start.14
  15.8 1.4 collective-permute-start.16
  17.2 1.4 collective-permute-start.18
  18.6 1.4 collective-permute-start.20
  20.1 1.4 collective-permute-start.22
  21.5 1.4 collective-permute-start.24
  22.9 55.5 %collective-permute-start.26 = (bf16[64,1024]{1,0:T(8,128)(2,1)S(1)}, bf16[64,1024]{1,0:T(8,128)(2,1)S(1)}, u32[]{:S(2)}, u32[]{:S(2)}) collective-permute-start(bf16[64,1024]{1,0:T(8,128)(2,1)S(1)} %top.31.refs_4_), channel_id=1, source_target_pairs={{13,14},{28,29},{43,44},{58,59},{73,74},{88,89},{103,104},{118,119... | collective-permute-start | bytes 393224 | tf_op jit(solution)/shard_map/while/body/eval_jaxpr/ppermute | solution.py:189
  24.2 54.2 %collective-permute-start.27 = (bf16[64,1024]{1,0:T(8,128)(2,1)S(1)}, bf16[64,1024]{1,0:T(8,128)(2,1)S(1)}, u32[]{:S(2)}, u32[]{:S(2)}) collective-permute-start(bf16[64,1024]{1,0:T(8,128)(2,1)S(1)} %right.31.refs_4_), channel_id=1, source_target_pairs={{13,29},{28,44},{43,59},{58,74},{73,89},{88,104},{103,119},{118,13... | collective-permute-start | bytes 393224 | tf_op jit(solution)/shard_map/while/body/eval_jaxpr/ppermute | solution.py:190
  78.4 5.4 %collective-permute-start.28 = (bf16[64,1024]{1,0:T(8,128)(2,1)S(1)}, bf16[64,1024]{1,0:T(8,128)(2,1)S(1)}, u32[]{:S(2)}, u32[]{:S(2)}) collective-permute-start(bf16[64,1024]{1,0:T(8,128)(2,1)S(1)} %top.32.refs_4_), channel_id=1, source_target_pairs={{14,15},{29,30},{44,45},{59,60},{74,75},{89,90},{104,105},{119,120... | collective-permute-start | bytes 393224 | tf_op jit(solution)/shard_map/while/body/eval_jaxpr/ppermute | solution.py:189
  79.1 8.1 %collective-permute-start.29 = (bf16[64,1024]{1,0:T(8,128)(2,1)S(1)}, bf16[64,1024]{1,0:T(8,128)(2,1)S(1)}, u32[]{:S(2)}, u32[]{:S(2)}) collective-permute-start(bf16[64,1024]{1,0:T(8,128)(2,1)S(1)} %right.32.after.refs_4_), channel_id=1, source_target_pairs={{14,30},{29,45},{44,60},{59,75},{74,90},{89,105},{104,120},{119,13... | collective-permute-start | bytes 393224 | tf_op jit(solution)/shard_map/while/body/eval_jaxpr/ppermute | solution.py:190
  87.2 4.7 %collective-permute-start = (bf16[64,1024]{1,0:T(8,128)(2,1)S(1)}, bf16[64,1024]{1,0:T(8,128)(2,1)S(1)}, u32[]{:S(2)}, u32[]{:S(2)}) collective-permute-start(bf16[64,1024]{1,0:T(8,128)(2,1)S(1)} %get-tuple-element.198.refs_4_), channel_id=1, source_target_pairs={{0,1},{30,31},{45,46},{60,61},{75,76},{90,91},{105,106},{120,121},... | collective-permute-start | bytes 393224 | tf_op jit(solution)/shard_map/while/body/eval_jaxpr/ppermute | solution.py:189
  87.9 4.0 %collective-permute-start.1 = (bf16[64,1024]{1,0:T(8,128)(2,1)S(1)}, bf16[64,1024]{1,0:T(8,128)(2,1)S(1)}, u32[]{:S(2)}, u32[]{:S(2)}) collective-permute-start(bf16[64,1024]{1,0:T(8,128)(2,1)S(1)} %get-tuple-element.197.refs_4_), channel_id=1, source_target_pairs={{0,16},{15,31},{30,46},{45,61},{60,76},{75,91},{90,106},{105,121},... | collective-permute-start | bytes 393224 | tf_op jit(solution)/shard_map/while/body/eval_jaxpr/ppermute | solution.py:190
  91.9 1.4 collective-permute-start.2
  93.3 1.4 collective-permute-start.4
  94.8 1.4 collective-permute-start.6
  96.2 1.4 collective-permute-start.8
  97.6 1.4 collective-permute-start.10
  99.1 1.4 collective-permute-start.12
  100.5 1.4 collective-permute-start.14
  101.9 1.4 collective-permute-start.16
  109.1 72.6 %collective-permute-start.26 = (bf16[64,1024]{1,0:T(8,128)(2,1)S(1)}, bf16[64,1024]{1,0:T(8,128)(2,1)S(1)}, u32[]{:S(2)}, u32[]{:S(2)}) collective-permute-start(bf16[64,1024]{1,0:T(8,128)(2,1)S(1)} %top.31.refs_4_), channel_id=1, source_target_pairs={{13,14},{28,29},{43,44},{58,59},{73,74},{88,89},{103,104},{118,119... | collective-permute-start | bytes 393224 | tf_op jit(solution)/shard_map/while/body/eval_jaxpr/ppermute | solution.py:189
  110.4 72.2 %collective-permute-start.27 = (bf16[64,1024]{1,0:T(8,128)(2,1)S(1)}, bf16[64,1024]{1,0:T(8,128)(2,1)S(1)}, u32[]{:S(2)}, u32[]{:S(2)}) collective-permute-start(bf16[64,1024]{1,0:T(8,128)(2,1)S(1)} %right.31.refs_4_), channel_id=1, source_target_pairs={{13,29},{28,44},{43,59},{58,74},{73,89},{88,104},{103,119},{118,13... | collective-permute-start | bytes 393224 | tf_op jit(solution)/shard_map/while/body/eval_jaxpr/ppermute | solution.py:190
  183.1 5.9 %collective-permute-start.28 = (bf16[64,1024]{1,0:T(8,128)(2,1)S(1)}, bf16[64,1024]{1,0:T(8,128)(2,1)S(1)}, u32[]{:S(2)}, u32[]{:S(2)}) collective-permute-start(bf16[64,1024]{1,0:T(8,128)(2,1)S(1)} %top.32.refs_4_), channel_id=1, source_target_pairs={{14,15},{29,30},{44,45},{59,60},{74,75},{89,90},{104,105},{119,120... | collective-permute-start | bytes 393224 | tf_op jit(solution)/shard_map/while/body/eval_jaxpr/ppermute | solution.py:189
  184.2 8.1 %collective-permute-start.29 = (bf16[64,1024]{1,0:T(8,128)(2,1)S(1)}, bf16[64,1024]{1,0:T(8,128)(2,1)S(1)}, u32[]{:S(2)}, u32[]{:S(2)}) collective-permute-start(bf16[64,1024]{1,0:T(8,128)(2,1)S(1)} %right.32.after.refs_4_), channel_id=1, source_target_pairs={{14,30},{29,45},{44,60},{59,75},{74,90},{89,105},{104,120},{119,13... | collective-permute-start | bytes 393224 | tf_op jit(solution)/shard_map/while/body/eval_jaxpr/ppermute | solution.py:190
  (34 other events, 201.3 us)

commit v5 on v4

--- a/solution.py
+++ b/solution.py
@@ -175,26 +175,28 @@
 def body(blocks, pattern, local_src, owner):
     nbatch, nsource, width = local_src.shape[2:]
     trace = width // 2
-    period = 15
+    period = 14
     nx, ny = lax.axis_size("gx"), lax.axis_size("gy")
     x, y = lax.axis_index("gx"), lax.axis_index("gy")
     source, right, top = sources((x * ny + y).reshape(1), owner, local_src[0, 0])
     position = (x + y).reshape(1)
 
-    def sweep(part, outs):
+    def sweep(part, outs, turns, again):
         right, top = outs
         ahead = position - part * period
         dense = assemble(ahead, pattern[0, 0], blocks[0, 0], width)
-        for turn in range(1, period + 1):
+        for turn in range(1, turns + 1):
             bottom = lax.ppermute(top, ("gx", "gy"), pairs(nx, ny, turn - 1, period, False))
             left = lax.ppermute(right, ("gx", "gy"), pairs(nx, ny, turn - 1, period, True))
-            after = [touch(dense, right)] if turn == period else []
+            after = [touch(dense, right)] if again and turn == turns else []
             total = first(turn, ahead, dense, source, bottom, *after)
             top = second(turn, 1, ahead, dense, total, left, top)
             right = second(turn, 0, ahead, dense, total, left, right)
         return right, top
 
-    right, top = lax.fori_loop(0, (nx + ny - 2) // period, sweep, (right, top))
+    parts, rest = divmod(nx + ny - 2, period)
+    outs = lax.fori_loop(0, parts, lambda part, outs: sweep(part, outs, period, True), (right, top))
+    right, top = sweep(parts, outs, rest, False)
     result = jnp.concatenate([right, top], axis=1)
     return result.reshape(1, 1, nbatch, nsource, width)
 

time: 194 us -> 190 us (0.979)
  waiting for transfers between devices: 123 us -> 113 us
  Pallas kernels: 10.2 us -> 13.5 us
    ppermute x30, waiting for transfers between devices: 123 us -> 109 us  [sweep(): lax.ppermute(top, ('gx', 'gy'), pairs(nx, ny, turn - 1, period, False))]
    ppermute x30, waiting for transfers between devices: 0.08 us -> 3.59 us  [sweep(): lax.ppermute(right, ('gx', 'gy'), pairs(nx, ny, turn - 1, period, True))]
    pallas_call x2 -> x3, Pallas kernels: 6.6 us -> 9.91 us  [assemble(): pl.pallas_call(assemble_kernel, out_shape=pltpu.VMEM((width, width), blk....]
  transfers between devices with their start and end apart: 60 -> 60, of which waited for: 2 -> 7; matrix products, arithmetic and copies ran while one was open for 0% -> 0% of each run, Pallas kernels for 4% -> 6%
where the time goes in v5:
time: 190 us; the launch traced here: 188 us
  waiting for transfers between devices  113 us (59%)
  starting transfers between devices  45.7 us (24%)
  Pallas kernels  13.5 us (7%)
  local copies, waits for them, and re-layouts  13.5 us (7%)
    ppermute x30, waiting for transfers between devices, sweep(): lax.ppermute(top, ('gx', 'gy'), pairs(nx, ny, turn - 1, period, False))  109 us
    ppermute x30, starting transfers between devices, sweep(): lax.ppermute(right, ('gx', 'gy'), pairs(nx, ny, turn - 1, period, True))  23.8 us
    ppermute x30, starting transfers between devices, sweep(): lax.ppermute(top, ('gx', 'gy'), pairs(nx, ny, turn - 1, period, False))  21.9 us
    while x12, local copies, waits for them, and re-layouts  13.5 us
    pallas_call x3, Pallas kernels, assemble(): pl.pallas_call(assemble_kernel, out_shape=pltpu.VMEM((width, width), blk....  9.91 us
  transfers between devices with their start and end apart: 60, of which 7 were waited for; matrix products, arithmetic and copies ran while one was open for 0% of the time, Pallas kernels for 6%

profile of v5, /device:TPU:254, one launch (start us, length us, event | category | flops | bytes accessed | tf_op | source)
XLA Modules:
  0.0 187.8 jit_solution(18014389186085819166)
XLA Ops:
  0.0 1.0 sources.1
  1.0 109.9 %while.15 = (s32[]{:T(128)}, bf16[64,1024]{1,0:T(8,128)(2,1)S(1)}, bf16[64,1024]{1,0:T(8,128)(2,1)S(1)}, s32[1]{0:T(128)}, s32[1,1,128]{2,1,0:T(1,128)}, /*index...) while((s32[]{:T(128)}, bf16[64,1024]{1,0:T(8,128)(2,1)S(1)}, ...), condition=%wide.region_1.0_spmd, body=%wide.region_0.0_spmd.sunk | while | flops 4 | bytes 115344688 | solution.py:198
  1.0 1.3 collective-permute-start
  2.3 1.3 collective-permute-start.1
  3.7 3.3 %assemble.3.refs_1_.dense = bf16[2048,2048]{1,0:T(8,128)(2,1)S(1)} custom-call(s32[1]{0:T(128)S(6)} %sub.15._.refs_0_, s32[128]{0:T(128)} %bitcast.18, bf16[128,128,128]{2,1,0:T(8,128)(2,1)} %bitcast.15), custom_call_target="tpu_custom_call" | custom-call | tf_op jit(solution)/shard_map/while/body/eval_jaxpr/assemble/pallas_call | solution.py:49
  7.0 0.9 collective-permute-done.refs_3_
  7.9 0.7 collective-permute-done.1.refs_3_
  9.3 1.3 collective-permute-start.3
  10.7 0.9 collective-permute-done.3.refs_3_
  12.3 0.7 collective-permute-start.5
  13.0 0.7 collective-permute-start.6
  13.7 0.7 collective-permute-start.7
  14.4 0.7 collective-permute-start.8
  15.1 0.7 collective-permute-start.9
  28.7 3.4 %copy-done.1 = bf16[2048,2048]{1,0:T(8,128)(2,1)S(1)} copy-done((bf16[2048,2048]{1,0:T(8,128)(2,1)S(1)}, bf16[2048,2048]{1,0:T(8,128)(2,1)}, u32[]{:S(2)}) %copy-start.1) | copy-done | bytes 8388632 | tf_op jit(solution)/shard_map/while
  32.1 3.4 %copy-done.2 = bf16[2048,2048]{1,0:T(8,128)(2,1)S(1)} copy-done((bf16[2048,2048]{1,0:T(8,128)(2,1)S(1)}, bf16[2048,2048]{1,0:T(8,128)(2,1)}, u32[]{:S(2)}) %copy-start.2) | copy-done | bytes 8388632 | tf_op jit(solution)/shard_map/while
  35.4 1.3 collective-permute-start
  36.7 1.3 collective-permute-start.1
  38.0 3.3 %assemble.3.refs_1_.dense = bf16[2048,2048]{1,0:T(8,128)(2,1)S(1)} custom-call(s32[1]{0:T(128)S(6)} %sub.15._.refs_0_, s32[128]{0:T(128)} %bitcast.18, bf16[128,128,128]{2,1,0:T(8,128)(2,1)} %bitcast.15), custom_call_target="tpu_custom_call" | custom-call | tf_op jit(solution)/shard_map/while/body/eval_jaxpr/assemble/pallas_call | solution.py:49
  41.4 42.7 %collective-permute-done.refs_3_ = bf16[64,1024]{1,0:T(8,128)(2,1)S(1)} collective-permute-done((bf16[64,1024]{1,0:T(8,128)(2,1)S(1)}, bf16[64,1024]{1,0:T(8,128)(2,1)S(1)}, u32[]{:S(2)}, u32[]{:S(2)}) %collective-permute-start) | collective-permute-done | bytes 131104 | tf_op jit(solution)/shard_map/while/body/eval_jaxpr/ppermute | solution.py:189
  84.8 1.3 collective-permute-start.3
  86.1 0.9 collective-permute-done.3.refs_3_
  104.2 3.4 %copy-done.1 = bf16[2048,2048]{1,0:T(8,128)(2,1)S(1)} copy-done((bf16[2048,2048]{1,0:T(8,128)(2,1)S(1)}, bf16[2048,2048]{1,0:T(8,128)(2,1)}, u32[]{:S(2)}) %copy-start.1) | copy-done | bytes 8388632 | tf_op jit(solution)/shard_map/while
  107.5 3.4 %copy-done.2 = bf16[2048,2048]{1,0:T(8,128)(2,1)S(1)} copy-done((bf16[2048,2048]{1,0:T(8,128)(2,1)S(1)}, bf16[2048,2048]{1,0:T(8,128)(2,1)}, u32[]{:S(2)}) %copy-start.2) | copy-done | bytes 8388632 | tf_op jit(solution)/shard_map/while
  110.9 1.3 collective-permute-start.28
  112.2 1.3 collective-permute-start.29
  113.5 3.3 %assemble.2.refs_1_ = bf16[2048,2048]{1,0:T(8,128)(2,1)S(1)} custom-call(s32[1]{0:T(128)S(6)} %sub.13._.refs_0_, s32[128]{0:T(128)} %bitcast.19, bf16[128,128,128]{2,1,0:T(8,128)(2,1)} %bitcast.16), custom_call_target="tpu_custom_call" | custom-call | tf_op jit(solution)/shard_map/assemble/pallas_call | solution.py:49
  116.8 65.5 %collective-permute-done.28.refs_3_ = bf16[64,1024]{1,0:T(8,128)(2,1)S(1)} collective-permute-done((bf16[64,1024]{1,0:T(8,128)(2,1)S(1)}, bf16[64,1024]{1,0:T(8,128)(2,1)S(1)}, u32[]{:S(2)}, u32[]{:S(2)}) %collective-permute-start.28) | collective-permute-done | bytes 131104 | tf_op jit(solution)/shard_map/ppermute | solution.py:189
  182.3 0.8 first.16.refs_2_
  184.8 1.3 collective-permute-start.31
  186.1 0.9 collective-permute-done.31.refs_3_
  187.1 0.7 pad_maximum_fusion
  (198 shorter events, 32.6 us)
Async XLA Ops:
  1.0 6.9 %collective-permute-start = (bf16[64,1024]{1,0:T(8,128)(2,1)S(1)}, bf16[64,1024]{1,0:T(8,128)(2,1)S(1)}, u32[]{:S(2)}, u32[]{:S(2)}) collective-permute-start(bf16[64,1024]{1,0:T(8,128)(2,1)S(1)} %get-tuple-element.198.refs_4_), channel_id=1, source_target_pairs={{0,1},{14,15},{29,30},{44,45},{59,60},{74,75},{89,90},{104,105},{1... | collective-permute-start | bytes 393224 | tf_op jit(solution)/shard_map/while/body/eval_jaxpr/ppermute | solution.py:189
  2.3 6.3 %collective-permute-start.1 = (bf16[64,1024]{1,0:T(8,128)(2,1)S(1)}, bf16[64,1024]{1,0:T(8,128)(2,1)S(1)}, u32[]{:S(2)}, u32[]{:S(2)}) collective-permute-start(bf16[64,1024]{1,0:T(8,128)(2,1)S(1)} %get-tuple-element.197.refs_4_), channel_id=1, source_target_pairs={{0,16},{14,30},{29,45},{44,60},{59,75},{74,90},{89,105},{104,120},... | collective-permute-start | bytes 393224 | tf_op jit(solution)/shard_map/while/body/eval_jaxpr/ppermute | solution.py:190
  8.6 2.0 %collective-permute-start.2 = (bf16[64,1024]{1,0:T(8,128)(2,1)S(1)}, bf16[64,1024]{1,0:T(8,128)(2,1)S(1)}, u32[]{:S(2)}, u32[]{:S(2)}) collective-permute-start(bf16[64,1024]{1,0:T(8,128)(2,1)S(1)} %top.22.refs_4_), channel_id=1, source_target_pairs={{1,2},{16,17},{30,31},{45,46},{60,61},{75,76},{90,91},{105,106},{1... | collective-permute-start | bytes 393224 | tf_op jit(solution)/shard_map/while/body/eval_jaxpr/ppermute | solution.py:189
  9.3 2.3 %collective-permute-start.3 = (bf16[64,1024]{1,0:T(8,128)(2,1)S(1)}, bf16[64,1024]{1,0:T(8,128)(2,1)S(1)}, u32[]{:S(2)}, u32[]{:S(2)}) collective-permute-start(bf16[64,1024]{1,0:T(8,128)(2,1)S(1)} %right.22.refs_4_), channel_id=1, source_target_pairs={{1,17},{15,31},{16,32},{30,46},{45,61},{60,76},{75,91},{90,106},{1... | collective-permute-start | bytes 393224 | tf_op jit(solution)/shard_map/while/body/eval_jaxpr/ppermute | solution.py:190
  13.0 1.4 collective-permute-start.6
  14.4 1.4 collective-permute-start.8
  15.9 1.4 collective-permute-start.10
  17.3 1.4 collective-permute-start.12
  18.7 1.4 collective-permute-start.14
  20.1 1.4 collective-permute-start.16
  21.6 1.4 collective-permute-start.18
  23.0 1.4 collective-permute-start.20
  24.4 1.4 collective-permute-start.22
  25.9 1.4 collective-permute-start.24
  27.3 4.8 %collective-permute-start.26 = (bf16[64,1024]{1,0:T(8,128)(2,1)S(1)}, bf16[64,1024]{1,0:T(8,128)(2,1)S(1)}, u32[]{:S(2)}, u32[]{:S(2)}) collective-permute-start(bf16[64,1024]{1,0:T(8,128)(2,1)S(1)} %top.34.refs_4_), channel_id=1, source_target_pairs={{13,14},{28,29},{43,44},{58,59},{73,74},{88,89},{103,104},{118,119... | collective-permute-start | bytes 393224 | tf_op jit(solution)/shard_map/while/body/eval_jaxpr/ppermute | solution.py:189
  28.0 7.4 %collective-permute-start.27 = (bf16[64,1024]{1,0:T(8,128)(2,1)S(1)}, bf16[64,1024]{1,0:T(8,128)(2,1)S(1)}, u32[]{:S(2)}, u32[]{:S(2)}) collective-permute-start(bf16[64,1024]{1,0:T(8,128)(2,1)S(1)} %right.34.after.refs_4_), channel_id=1, source_target_pairs={{13,29},{28,44},{43,59},{58,74},{73,89},{88,104},{103,119},{118,13... | collective-permute-start | bytes 393224 | tf_op jit(solution)/shard_map/while/body/eval_jaxpr/ppermute | solution.py:190
  35.4 48.7 %collective-permute-start = (bf16[64,1024]{1,0:T(8,128)(2,1)S(1)}, bf16[64,1024]{1,0:T(8,128)(2,1)S(1)}, u32[]{:S(2)}, u32[]{:S(2)}) collective-permute-start(bf16[64,1024]{1,0:T(8,128)(2,1)S(1)} %get-tuple-element.198.refs_4_), channel_id=1, source_target_pairs={{0,1},{14,15},{29,30},{44,45},{59,60},{74,75},{89,90},{104,105},{1... | collective-permute-start | bytes 393224 | tf_op jit(solution)/shard_map/while/body/eval_jaxpr/ppermute | solution.py:189
  36.7 47.4 %collective-permute-start.1 = (bf16[64,1024]{1,0:T(8,128)(2,1)S(1)}, bf16[64,1024]{1,0:T(8,128)(2,1)S(1)}, u32[]{:S(2)}, u32[]{:S(2)}) collective-permute-start(bf16[64,1024]{1,0:T(8,128)(2,1)S(1)} %get-tuple-element.197.refs_4_), channel_id=1, source_target_pairs={{0,16},{14,30},{29,45},{44,60},{59,75},{74,90},{89,105},{104,120},... | collective-permute-start | bytes 393224 | tf_op jit(solution)/shard_map/while/body/eval_jaxpr/ppermute | solution.py:190
  84.1 2.0 %collective-permute-start.2 = (bf16[64,1024]{1,0:T(8,128)(2,1)S(1)}, bf16[64,1024]{1,0:T(8,128)(2,1)S(1)}, u32[]{:S(2)}, u32[]{:S(2)}) collective-permute-start(bf16[64,1024]{1,0:T(8,128)(2,1)S(1)} %top.22.refs_4_), channel_id=1, source_target_pairs={{1,2},{16,17},{30,31},{45,46},{60,61},{75,76},{90,91},{105,106},{1... | collective-permute-start | bytes 393224 | tf_op jit(solution)/shard_map/while/body/eval_jaxpr/ppermute | solution.py:189
  84.8 2.3 %collective-permute-start.3 = (bf16[64,1024]{1,0:T(8,128)(2,1)S(1)}, bf16[64,1024]{1,0:T(8,128)(2,1)S(1)}, u32[]{:S(2)}, u32[]{:S(2)}) collective-permute-start(bf16[64,1024]{1,0:T(8,128)(2,1)S(1)} %right.22.refs_4_), channel_id=1, source_target_pairs={{1,17},{15,31},{16,32},{30,46},{45,61},{60,76},{75,91},{90,106},{1... | collective-permute-start | bytes 393224 | tf_op jit(solution)/shard_map/while/body/eval_jaxpr/ppermute | solution.py:190
  88.5 1.4 collective-permute-start.6
  89.9 1.4 collective-permute-start.8
  91.3 1.4 collective-permute-start.10
  92.8 1.4 collective-permute-start.12
  94.2 1.4 collective-permute-start.14
  95.6 1.4 collective-permute-start.16
  102.8 4.8 %collective-permute-start.26 = (bf16[64,1024]{1,0:T(8,128)(2,1)S(1)}, bf16[64,1024]{1,0:T(8,128)(2,1)S(1)}, u32[]{:S(2)}, u32[]{:S(2)}) collective-permute-start(bf16[64,1024]{1,0:T(8,128)(2,1)S(1)} %top.34.refs_4_), channel_id=1, source_target_pairs={{13,14},{28,29},{43,44},{58,59},{73,74},{88,89},{103,104},{118,119... | collective-permute-start | bytes 393224 | tf_op jit(solution)/shard_map/while/body/eval_jaxpr/ppermute | solution.py:189
  103.5 7.4 %collective-permute-start.27 = (bf16[64,1024]{1,0:T(8,128)(2,1)S(1)}, bf16[64,1024]{1,0:T(8,128)(2,1)S(1)}, u32[]{:S(2)}, u32[]{:S(2)}) collective-permute-start(bf16[64,1024]{1,0:T(8,128)(2,1)S(1)} %right.34.after.refs_4_), channel_id=1, source_target_pairs={{13,29},{28,44},{43,59},{58,74},{73,89},{88,104},{103,119},{118,13... | collective-permute-start | bytes 393224 | tf_op jit(solution)/shard_map/while/body/eval_jaxpr/ppermute | solution.py:190
  110.9 71.4 %collective-permute-start.28 = (bf16[64,1024]{1,0:T(8,128)(2,1)S(1)}, bf16[64,1024]{1,0:T(8,128)(2,1)S(1)}, u32[]{:S(2)}, u32[]{:S(2)}) collective-permute-start(bf16[64,1024]{1,0:T(8,128)(2,1)S(1)} %get-tuple-element.128.refs_4_), channel_id=1, source_target_pairs={{0,1},{14,15},{29,30},{44,45},{59,60},{74,75},{89,90},{104,105},{1... | collective-permute-start | bytes 393224 | tf_op jit(solution)/shard_map/ppermute | solution.py:189
  112.2 70.9 %collective-permute-start.29 = (bf16[64,1024]{1,0:T(8,128)(2,1)S(1)}, bf16[64,1024]{1,0:T(8,128)(2,1)S(1)}, u32[]{:S(2)}, u32[]{:S(2)}) collective-permute-start(bf16[64,1024]{1,0:T(8,128)(2,1)S(1)} %get-tuple-element.129.refs_4_), channel_id=1, source_target_pairs={{0,16},{14,30},{29,45},{44,60},{59,75},{74,90},{89,105},{104,120},... | collective-permute-start | bytes 393224 | tf_op jit(solution)/shard_map/ppermute | solution.py:190
  183.6 2.5 %collective-permute-start.30 = (bf16[64,1024]{1,0:T(8,128)(2,1)S(1)}, bf16[64,1024]{1,0:T(8,128)(2,1)S(1)}, u32[]{:S(2)}, u32[]{:S(2)}) collective-permute-start(bf16[64,1024]{1,0:T(8,128)(2,1)S(1)} %top.20.refs_4_), channel_id=1, source_target_pairs={{1,2},{16,17},{30,31},{45,46},{60,61},{75,76},{90,91},{105,106},{1... | collective-permute-start | bytes 393224 | tf_op jit(solution)/shard_map/ppermute | solution.py:189
  184.8 2.3 %collective-permute-start.31 = (bf16[64,1024]{1,0:T(8,128)(2,1)S(1)}, bf16[64,1024]{1,0:T(8,128)(2,1)S(1)}, u32[]{:S(2)}, u32[]{:S(2)}) collective-permute-start(bf16[64,1024]{1,0:T(8,128)(2,1)S(1)} %right.20.refs_4_), channel_id=1, source_target_pairs={{1,17},{15,31},{16,32},{30,46},{45,61},{60,76},{75,91},{90,106},{1... | collective-permute-start | bytes 393224 | tf_op jit(solution)/shard_map/ppermute | solution.py:190
  (34 other events, 120.4 us)

commit v6 on v5

--- a/solution.py
+++ b/solution.py
@@ -120,26 +120,26 @@
     )(dense, after)
 
 
-def first_kernel(turn, position, dense, source, bottom, *refs):
+def first_kernel(turn, position, dense, source, left, *refs):
     total = refs[-1]
 
+    @pl.when(position[0] == turn)
+    def _():
+        trace = left.shape[1]
+        part = jnp.dot(left[...], dense[:trace], preferred_element_type=jnp.float32)
+        total[...] = part + source[...].astype(jnp.float32)
+
+
+def second_kernel(turn, half, position, dense, total, bottom, _, out):
     @pl.when(position[0] == turn)
     def _():
         trace = bottom.shape[1]
-        part = jnp.dot(bottom[...], dense[trace:], preferred_element_type=jnp.float32)
-        total[...] = part + source[...].astype(jnp.float32)
-
-
-def second_kernel(turn, half, position, dense, total, left, _, out):
-    @pl.when(position[0] == turn)
-    def _():
-        trace = left.shape[1]
         cols = slice(half * trace, (half + 1) * trace)
-        part = jnp.dot(left[...], dense[:trace, cols], preferred_element_type=jnp.float32)
+        part = jnp.dot(bottom[...], dense[trace:, cols], preferred_element_type=jnp.float32)
         out[...] = (total[:, cols] + part).astype(out.dtype)
 
 
-def first(turn, position, dense, source, bottom, *after):
+def first(turn, position, dense, source, left, *after):
     return pl.pallas_call(
         lambda *refs: first_kernel(turn, *refs),
         out_shape=pltpu.VMEM(source.shape, jnp.float32),
@@ -147,10 +147,10 @@
         out_specs=VMEM,
         compiler_params=PARAMS,
         name="first",
-    )(position, dense, source, bottom, *after)
-
-
-def second(turn, half, position, dense, total, left, out):
+    )(position, dense, source, left, *after)
+
+
+def second(turn, half, position, dense, total, bottom, out):
     return pl.pallas_call(
         lambda *refs: second_kernel(turn, half, *refs),
         out_shape=jax.ShapeDtypeStruct(out.shape, out.dtype),
@@ -159,7 +159,7 @@
         input_output_aliases={4: 0},
         compiler_params=PARAMS,
         name="right" if half == 0 else "top",
-    )(position, dense, total, left, out)
+    )(position, dense, total, bottom, out)
 
 
 def pairs(nx, ny, turn, period, across):
@@ -186,12 +186,12 @@
         ahead = position - part * period
         dense = assemble(ahead, pattern[0, 0], blocks[0, 0], width)
         for turn in range(1, turns + 1):
+            left = lax.ppermute(right, ("gx", "gy"), pairs(nx, ny, turn - 1, period, True))
             bottom = lax.ppermute(top, ("gx", "gy"), pairs(nx, ny, turn - 1, period, False))
-            left = lax.ppermute(right, ("gx", "gy"), pairs(nx, ny, turn - 1, period, True))
-            after = [touch(dense, right)] if again and turn == turns else []
-            total = first(turn, ahead, dense, source, bottom, *after)
-            top = second(turn, 1, ahead, dense, total, left, top)
-            right = second(turn, 0, ahead, dense, total, left, right)
+            after = [touch(dense, top)] if again and turn == turns else []
+            total = first(turn, ahead, dense, source, left, *after)
+            right = second(turn, 0, ahead, dense, total, bottom, right)
+            top = second(turn, 1, ahead, dense, total, bottom, top)
         return right, top
 
     parts, rest = divmod(nx + ny - 2, period)

time: 190 us -> 192 us (1.011)
    ppermute x30, waiting for transfers between devices: 3.59 us -> 106 us  [sweep(): lax.ppermute(right, ('gx', 'gy'), pairs(nx, ny, turn - 1, period, True))]
    ppermute x30, waiting for transfers between devices: 109 us -> 7.49 us  [sweep(): lax.ppermute(top, ('gx', 'gy'), pairs(nx, ny, turn - 1, period, False))]
where the time goes in v6:
time: 192 us; the launch traced here: 188 us
  waiting for transfers between devices  113 us (59%)
  starting transfers between devices  45.7 us (24%)
  Pallas kernels  13.5 us (7%)
  local copies, waits for them, and re-layouts  13.5 us (7%)
    ppermute x30, waiting for transfers between devices, sweep(): lax.ppermute(right, ('gx', 'gy'), pairs(nx, ny, turn - 1, period, True))  106 us
    ppermute x30, starting transfers between devices, sweep(): lax.ppermute(right, ('gx', 'gy'), pairs(nx, ny, turn - 1, period, True))  23.8 us
    ppermute x30, starting transfers between devices, sweep(): lax.ppermute(top, ('gx', 'gy'), pairs(nx, ny, turn - 1, period, False))  21.9 us
    while x12, local copies, waits for them, and re-layouts  13.5 us
    pallas_call x3, Pallas kernels, assemble(): pl.pallas_call(assemble_kernel, out_shape=pltpu.VMEM((width, width), blk....  9.91 us
    ppermute x30, waiting for transfers between devices, sweep(): lax.ppermute(top, ('gx', 'gy'), pairs(nx, ny, turn - 1, period, False))  7.49 us
  transfers between devices with their start and end apart: 60, of which 7 were waited for; matrix products, arithmetic and copies ran while one was open for 0% of the time, Pallas kernels for 6%

profile of v6, /device:TPU:254, one launch (start us, length us, event | category | flops | bytes accessed | tf_op | source)
XLA Modules:
  0.0 188.3 jit_solution(11702258840354749535)
XLA Ops:
  0.0 1.0 sources.1
  1.0 126.0 %while.15 = (s32[]{:T(128)}, bf16[64,1024]{1,0:T(8,128)(2,1)S(1)}, bf16[64,1024]{1,0:T(8,128)(2,1)S(1)}, s32[1]{0:T(128)}, s32[1,1,128]{2,1,0:T(1,128)}, /*index...) while((s32[]{:T(128)}, bf16[64,1024]{1,0:T(8,128)(2,1)S(1)}, ...), condition=%wide.region_1.0_spmd, body=%wide.region_0.0_spmd.sunk | while | flops 4 | bytes 115344688 | solution.py:198
  1.0 1.3 collective-permute-start
  2.3 1.3 collective-permute-start.1
  3.7 3.3 %assemble.3.refs_1_.dense = bf16[2048,2048]{1,0:T(8,128)(2,1)S(1)} custom-call(s32[1]{0:T(128)S(6)} %sub.15._.refs_0_, s32[128]{0:T(128)} %bitcast.18, bf16[128,128,128]{2,1,0:T(8,128)(2,1)} %bitcast.15), custom_call_target="tpu_custom_call" | custom-call | tf_op jit(solution)/shard_map/while/body/eval_jaxpr/assemble/pallas_call | solution.py:49
  7.3 1.9 collective-permute-done.1.refs_3_
  9.2 1.3 collective-permute-start.2
  21.5 0.7 collective-permute-start.18
  22.9 0.7 collective-permute-start.20
  24.3 0.7 collective-permute-start.22
  25.7 0.7 collective-permute-start.24
  26.4 0.7 collective-permute-start.25
  27.2 0.7 collective-permute-start.26
  27.9 0.7 collective-permute-start.27
  28.6 3.4 %copy-done.1 = bf16[2048,2048]{1,0:T(8,128)(2,1)S(1)} copy-done((bf16[2048,2048]{1,0:T(8,128)(2,1)S(1)}, bf16[2048,2048]{1,0:T(8,128)(2,1)}, u32[]{:S(2)}) %copy-start.1) | copy-done | bytes 8388632 | tf_op jit(solution)/shard_map/while
  31.9 3.4 %copy-done.2 = bf16[2048,2048]{1,0:T(8,128)(2,1)S(1)} copy-done((bf16[2048,2048]{1,0:T(8,128)(2,1)S(1)}, bf16[2048,2048]{1,0:T(8,128)(2,1)}, u32[]{:S(2)}) %copy-start.2) | copy-done | bytes 8388632 | tf_op jit(solution)/shard_map/while
  35.3 1.3 collective-permute-start
  36.6 1.3 collective-permute-start.1
  37.9 3.3 %assemble.3.refs_1_.dense = bf16[2048,2048]{1,0:T(8,128)(2,1)S(1)} custom-call(s32[1]{0:T(128)S(6)} %sub.15._.refs_0_, s32[128]{0:T(128)} %bitcast.18, bf16[128,128,128]{2,1,0:T(8,128)(2,1)} %bitcast.15), custom_call_target="tpu_custom_call" | custom-call | tf_op jit(solution)/shard_map/while/body/eval_jaxpr/assemble/pallas_call | solution.py:49
  41.2 54.1 %collective-permute-done.refs_3_ = bf16[64,1024]{1,0:T(8,128)(2,1)S(1)} collective-permute-done((bf16[64,1024]{1,0:T(8,128)(2,1)S(1)}, bf16[64,1024]{1,0:T(8,128)(2,1)S(1)}, u32[]{:S(2)}, u32[]{:S(2)}) %collective-permute-start) | collective-permute-done | bytes 131104 | tf_op jit(solution)/shard_map/while/body/eval_jaxpr/ppermute | solution.py:189
  95.4 5.5 %collective-permute-done.1.refs_3_ = bf16[64,1024]{1,0:T(8,128)(2,1)S(1)} collective-permute-done((bf16[64,1024]{1,0:T(8,128)(2,1)S(1)}, bf16[64,1024]{1,0:T(8,128)(2,1)S(1)}, u32[]{:S(2)}, u32[]{:S(2)}) %collective-permute-start.1) | collective-permute-done | bytes 131104 | tf_op jit(solution)/shard_map/while/body/eval_jaxpr/ppermute | solution.py:190
  100.9 1.3 collective-permute-start.2
  102.2 0.7 collective-permute-start.3
  120.3 3.4 %copy-done.1 = bf16[2048,2048]{1,0:T(8,128)(2,1)S(1)} copy-done((bf16[2048,2048]{1,0:T(8,128)(2,1)S(1)}, bf16[2048,2048]{1,0:T(8,128)(2,1)}, u32[]{:S(2)}) %copy-start.1) | copy-done | bytes 8388632 | tf_op jit(solution)/shard_map/while
  123.6 3.4 %copy-done.2 = bf16[2048,2048]{1,0:T(8,128)(2,1)S(1)} copy-done((bf16[2048,2048]{1,0:T(8,128)(2,1)S(1)}, bf16[2048,2048]{1,0:T(8,128)(2,1)}, u32[]{:S(2)}) %copy-start.2) | copy-done | bytes 8388632 | tf_op jit(solution)/shard_map/while
  127.0 1.3 collective-permute-start.28
  128.3 1.3 collective-permute-start.29
  129.6 3.3 %assemble.2.refs_1_ = bf16[2048,2048]{1,0:T(8,128)(2,1)S(1)} custom-call(s32[1]{0:T(128)S(6)} %sub.13._.refs_0_, s32[128]{0:T(128)} %bitcast.19, bf16[128,128,128]{2,1,0:T(8,128)(2,1)} %bitcast.16), custom_call_target="tpu_custom_call" | custom-call | tf_op jit(solution)/shard_map/assemble/pallas_call | solution.py:49
  132.9 50.7 %collective-permute-done.28.refs_3_ = bf16[64,1024]{1,0:T(8,128)(2,1)S(1)} collective-permute-done((bf16[64,1024]{1,0:T(8,128)(2,1)S(1)}, bf16[64,1024]{1,0:T(8,128)(2,1)S(1)}, u32[]{:S(2)}, u32[]{:S(2)}) %collective-permute-start.28) | collective-permute-done | bytes 131104 | tf_op jit(solution)/shard_map/ppermute | solution.py:189
  183.7 0.8 first.16.refs_2_
  185.0 1.3 collective-permute-start.30
  187.6 0.7 pad_maximum_fusion
  (198 shorter events, 31.5 us)
Async XLA Ops:
  1.0 6.3 %collective-permute-start = (bf16[64,1024]{1,0:T(8,128)(2,1)S(1)}, bf16[64,1024]{1,0:T(8,128)(2,1)S(1)}, u32[]{:S(2)}, u32[]{:S(2)}) collective-permute-start(bf16[64,1024]{1,0:T(8,128)(2,1)S(1)} %get-tuple-element.197.refs_4_), channel_id=1, source_target_pairs={{0,16},{14,30},{29,45},{44,60},{59,75},{74,90},{89,105},{104,120},... | collective-permute-start | bytes 393224 | tf_op jit(solution)/shard_map/while/body/eval_jaxpr/ppermute | solution.py:189
  2.3 6.9 %collective-permute-start.1 = (bf16[64,1024]{1,0:T(8,128)(2,1)S(1)}, bf16[64,1024]{1,0:T(8,128)(2,1)S(1)}, u32[]{:S(2)}, u32[]{:S(2)}) collective-permute-start(bf16[64,1024]{1,0:T(8,128)(2,1)S(1)} %get-tuple-element.198.refs_4_), channel_id=1, source_target_pairs={{0,1},{14,15},{29,30},{44,45},{59,60},{74,75},{89,90},{104,105},{1... | collective-permute-start | bytes 393224 | tf_op jit(solution)/shard_map/while/body/eval_jaxpr/ppermute | solution.py:190
  9.2 2.3 %collective-permute-start.2 = (bf16[64,1024]{1,0:T(8,128)(2,1)S(1)}, bf16[64,1024]{1,0:T(8,128)(2,1)S(1)}, u32[]{:S(2)}, u32[]{:S(2)}) collective-permute-start(bf16[64,1024]{1,0:T(8,128)(2,1)S(1)} %right.22.refs_4_), channel_id=1, source_target_pairs={{1,17},{15,31},{16,32},{30,46},{45,61},{60,76},{75,91},{90,106},{1... | collective-permute-start | bytes 393224 | tf_op jit(solution)/shard_map/while/body/eval_jaxpr/ppermute | solution.py:189
  12.9 1.4 collective-permute-start.6
  14.3 1.4 collective-permute-start.8
  17.2 1.4 collective-permute-start.12
  18.6 1.4 collective-permute-start.14
  20.0 1.4 collective-permute-start.16
  21.5 1.4 collective-permute-start.18
  22.9 1.4 collective-permute-start.20
  24.3 1.4 collective-permute-start.22
  25.7 1.4 collective-permute-start.24
  27.2 4.8 %collective-permute-start.26 = (bf16[64,1024]{1,0:T(8,128)(2,1)S(1)}, bf16[64,1024]{1,0:T(8,128)(2,1)S(1)}, u32[]{:S(2)}, u32[]{:S(2)}) collective-permute-start(bf16[64,1024]{1,0:T(8,128)(2,1)S(1)} %right.34.refs_4_), channel_id=1, source_target_pairs={{13,29},{28,44},{43,59},{58,74},{73,89},{88,104},{103,119},{118,13... | collective-permute-start | bytes 393224 | tf_op jit(solution)/shard_map/while/body/eval_jaxpr/ppermute | solution.py:189
  27.9 7.4 %collective-permute-start.27 = (bf16[64,1024]{1,0:T(8,128)(2,1)S(1)}, bf16[64,1024]{1,0:T(8,128)(2,1)S(1)}, u32[]{:S(2)}, u32[]{:S(2)}) collective-permute-start(bf16[64,1024]{1,0:T(8,128)(2,1)S(1)} %top.34.after.refs_4_), channel_id=1, source_target_pairs={{13,14},{28,29},{43,44},{58,59},{73,74},{88,89},{103,104},{118,119... | collective-permute-start | bytes 393224 | tf_op jit(solution)/shard_map/while/body/eval_jaxpr/ppermute | solution.py:190
  35.3 60.0 %collective-permute-start = (bf16[64,1024]{1,0:T(8,128)(2,1)S(1)}, bf16[64,1024]{1,0:T(8,128)(2,1)S(1)}, u32[]{:S(2)}, u32[]{:S(2)}) collective-permute-start(bf16[64,1024]{1,0:T(8,128)(2,1)S(1)} %get-tuple-element.197.refs_4_), channel_id=1, source_target_pairs={{0,16},{14,30},{29,45},{44,60},{59,75},{74,90},{89,105},{104,120},... | collective-permute-start | bytes 393224 | tf_op jit(solution)/shard_map/while/body/eval_jaxpr/ppermute | solution.py:189
  36.6 64.3 %collective-permute-start.1 = (bf16[64,1024]{1,0:T(8,128)(2,1)S(1)}, bf16[64,1024]{1,0:T(8,128)(2,1)S(1)}, u32[]{:S(2)}, u32[]{:S(2)}) collective-permute-start(bf16[64,1024]{1,0:T(8,128)(2,1)S(1)} %get-tuple-element.198.refs_4_), channel_id=1, source_target_pairs={{0,1},{14,15},{29,30},{44,45},{59,60},{74,75},{89,90},{104,105},{1... | collective-permute-start | bytes 393224 | tf_op jit(solution)/shard_map/while/body/eval_jaxpr/ppermute | solution.py:190
  100.9 2.3 %collective-permute-start.2 = (bf16[64,1024]{1,0:T(8,128)(2,1)S(1)}, bf16[64,1024]{1,0:T(8,128)(2,1)S(1)}, u32[]{:S(2)}, u32[]{:S(2)}) collective-permute-start(bf16[64,1024]{1,0:T(8,128)(2,1)S(1)} %right.22.refs_4_), channel_id=1, source_target_pairs={{1,17},{15,31},{16,32},{30,46},{45,61},{60,76},{75,91},{90,106},{1... | collective-permute-start | bytes 393224 | tf_op jit(solution)/shard_map/while/body/eval_jaxpr/ppermute | solution.py:189
  104.6 1.4 collective-permute-start.6
  106.0 1.4 collective-permute-start.8
  107.4 1.4 collective-permute-start.10
  108.9 1.4 collective-permute-start.12
  110.3 1.4 collective-permute-start.14
  111.7 1.4 collective-permute-start.16
  113.2 1.4 collective-permute-start.18
  114.6 1.4 collective-permute-start.20
  116.0 1.4 collective-permute-start.22
  117.4 1.4 collective-permute-start.24
  118.9 4.8 %collective-permute-start.26 = (bf16[64,1024]{1,0:T(8,128)(2,1)S(1)}, bf16[64,1024]{1,0:T(8,128)(2,1)S(1)}, u32[]{:S(2)}, u32[]{:S(2)}) collective-permute-start(bf16[64,1024]{1,0:T(8,128)(2,1)S(1)} %right.34.refs_4_), channel_id=1, source_target_pairs={{13,29},{28,44},{43,59},{58,74},{73,89},{88,104},{103,119},{118,13... | collective-permute-start | bytes 393224 | tf_op jit(solution)/shard_map/while/body/eval_jaxpr/ppermute | solution.py:189
  119.6 7.4 %collective-permute-start.27 = (bf16[64,1024]{1,0:T(8,128)(2,1)S(1)}, bf16[64,1024]{1,0:T(8,128)(2,1)S(1)}, u32[]{:S(2)}, u32[]{:S(2)}) collective-permute-start(bf16[64,1024]{1,0:T(8,128)(2,1)S(1)} %top.34.after.refs_4_), channel_id=1, source_target_pairs={{13,14},{28,29},{43,44},{58,59},{73,74},{88,89},{103,104},{118,119... | collective-permute-start | bytes 393224 | tf_op jit(solution)/shard_map/while/body/eval_jaxpr/ppermute | solution.py:190
  127.0 56.6 %collective-permute-start.28 = (bf16[64,1024]{1,0:T(8,128)(2,1)S(1)}, bf16[64,1024]{1,0:T(8,128)(2,1)S(1)}, u32[]{:S(2)}, u32[]{:S(2)}) collective-permute-start(bf16[64,1024]{1,0:T(8,128)(2,1)S(1)} %get-tuple-element.128.refs_4_), channel_id=1, source_target_pairs={{0,16},{14,30},{29,45},{44,60},{59,75},{74,90},{89,105},{104,120},... | collective-permute-start | bytes 393224 | tf_op jit(solution)/shard_map/ppermute | solution.py:189
  128.3 56.2 %collective-permute-start.29 = (bf16[64,1024]{1,0:T(8,128)(2,1)S(1)}, bf16[64,1024]{1,0:T(8,128)(2,1)S(1)}, u32[]{:S(2)}, u32[]{:S(2)}) collective-permute-start(bf16[64,1024]{1,0:T(8,128)(2,1)S(1)} %get-tuple-element.129.refs_4_), channel_id=1, source_target_pairs={{0,1},{14,15},{29,30},{44,45},{59,60},{74,75},{89,90},{104,105},{1... | collective-permute-start | bytes 393224 | tf_op jit(solution)/shard_map/ppermute | solution.py:190
  185.0 2.5 %collective-permute-start.30 = (bf16[64,1024]{1,0:T(8,128)(2,1)S(1)}, bf16[64,1024]{1,0:T(8,128)(2,1)S(1)}, u32[]{:S(2)}, u32[]{:S(2)}) collective-permute-start(bf16[64,1024]{1,0:T(8,128)(2,1)S(1)} %right.20.refs_4_), channel_id=1, source_target_pairs={{1,17},{15,31},{16,32},{30,46},{45,61},{60,76},{75,91},{90,106},{1... | collective-permute-start | bytes 393224 | tf_op jit(solution)/shard_map/ppermute | solution.py:189
  (34 other events, 135.0 us)

commit v7 on v5

--- a/solution.py
+++ b/solution.py
@@ -175,7 +175,7 @@
 def body(blocks, pattern, local_src, owner):
     nbatch, nsource, width = local_src.shape[2:]
     trace = width // 2
-    period = 14
+    period = 12
     nx, ny = lax.axis_size("gx"), lax.axis_size("gy")
     x, y = lax.axis_index("gx"), lax.axis_index("gy")
     source, right, top = sources((x * ny + y).reshape(1), owner, local_src[0, 0])

time: 190 us -> 190 us (level)
  transfers between devices with their start and end apart: 60 -> 60, of which waited for: 7 -> 6; matrix products, arithmetic and copies ran while one was open for 0% -> 0% of each run, Pallas kernels for 6% -> 6%
where the time goes in v7:
time: 190 us; the launch traced here: 188 us
  waiting for transfers between devices  113 us (59%)
  starting transfers between devices  45.7 us (24%)
  Pallas kernels  13.5 us (7%)
  local copies, waits for them, and re-layouts  13.5 us (7%)
    ppermute x30, waiting for transfers between devices, sweep(): lax.ppermute(top, ('gx', 'gy'), pairs(nx, ny, turn - 1, period, False))  110 us
    ppermute x30, starting transfers between devices, sweep(): lax.ppermute(right, ('gx', 'gy'), pairs(nx, ny, turn - 1, period, True))  23.8 us
    ppermute x30, starting transfers between devices, sweep(): lax.ppermute(top, ('gx', 'gy'), pairs(nx, ny, turn - 1, period, False))  21.9 us
    while x12, local copies, waits for them, and re-layouts  13.5 us
    pallas_call x3, Pallas kernels, assemble(): pl.pallas_call(assemble_kernel, out_shape=pltpu.VMEM((width, width), blk....  9.92 us
  transfers between devices with their start and end apart: 60, of which 6 were waited for; matrix products, arithmetic and copies ran while one was open for 0% of the time, Pallas kernels for 6%

profile of v7, /device:TPU:254, one launch (start us, length us, event | category | flops | bytes accessed | tf_op | source)
XLA Modules:
  0.0 187.7 jit_solution(10847310204599919207)
XLA Ops:
  0.0 1.0 sources.1
  1.0 110.6 %while.15 = (s32[]{:T(128)}, bf16[64,1024]{1,0:T(8,128)(2,1)S(1)}, bf16[64,1024]{1,0:T(8,128)(2,1)S(1)}, s32[1]{0:T(128)}, s32[1,1,128]{2,1,0:T(1,128)}, /*index...) while((s32[]{:T(128)}, bf16[64,1024]{1,0:T(8,128)(2,1)S(1)}, ...), condition=%wide.region_1.0_spmd, body=%wide.region_0.0_spmd.sunk | while | flops 4 | bytes 113247376 | solution.py:198
  2.4 3.3 %assemble.3.refs_1_.dense = bf16[2048,2048]{1,0:T(8,128)(2,1)S(1)} custom-call(s32[1]{0:T(128)S(6)} %sub.15._.refs_0_, s32[128]{0:T(128)} %bitcast.18, bf16[128,128,128]{2,1,0:T(8,128)(2,1)} %bitcast.15), custom_call_target="tpu_custom_call" | custom-call | tf_op jit(solution)/shard_map/while/body/eval_jaxpr/assemble/pallas_call | solution.py:49
  5.8 0.7 collective-permute-start.2
  6.5 0.7 collective-permute-start.3
  7.9 0.7 collective-permute-start.5
  9.3 0.7 collective-permute-start.7
  10.1 1.3 collective-permute-start.8
  11.4 1.3 collective-permute-start.9
  12.7 17.3 %collective-permute-done.8.refs_3_ = bf16[64,1024]{1,0:T(8,128)(2,1)S(1)} collective-permute-done((bf16[64,1024]{1,0:T(8,128)(2,1)S(1)}, bf16[64,1024]{1,0:T(8,128)(2,1)S(1)}, u32[]{:S(2)}, u32[]{:S(2)}) %collective-permute-start.8) | collective-permute-done | bytes 131104 | tf_op jit(solution)/shard_map/while/body/eval_jaxpr/ppermute | solution.py:189
  30.7 1.3 collective-permute-start.11
  32.0 0.9 collective-permute-done.11.refs_3_
  34.4 0.7 collective-permute-start.14
  35.1 0.7 collective-permute-start.15
  41.5 3.4 %copy-done.1 = bf16[2048,2048]{1,0:T(8,128)(2,1)S(1)} copy-done((bf16[2048,2048]{1,0:T(8,128)(2,1)S(1)}, bf16[2048,2048]{1,0:T(8,128)(2,1)}, u32[]{:S(2)}) %copy-start.1) | copy-done | bytes 8388632 | tf_op jit(solution)/shard_map/while
  44.9 3.4 %copy-done.2 = bf16[2048,2048]{1,0:T(8,128)(2,1)S(1)} copy-done((bf16[2048,2048]{1,0:T(8,128)(2,1)S(1)}, bf16[2048,2048]{1,0:T(8,128)(2,1)}, u32[]{:S(2)}) %copy-start.2) | copy-done | bytes 8388632 | tf_op jit(solution)/shard_map/while
  49.6 3.3 %assemble.3.refs_1_.dense = bf16[2048,2048]{1,0:T(8,128)(2,1)S(1)} custom-call(s32[1]{0:T(128)S(6)} %sub.15._.refs_0_, s32[128]{0:T(128)} %bitcast.18, bf16[128,128,128]{2,1,0:T(8,128)(2,1)} %bitcast.15), custom_call_target="tpu_custom_call" | custom-call | tf_op jit(solution)/shard_map/while/body/eval_jaxpr/assemble/pallas_call | solution.py:49
  57.3 1.3 collective-permute-start.8
  58.6 1.3 collective-permute-start.9
  59.9 33.5 %collective-permute-done.8.refs_3_ = bf16[64,1024]{1,0:T(8,128)(2,1)S(1)} collective-permute-done((bf16[64,1024]{1,0:T(8,128)(2,1)S(1)}, bf16[64,1024]{1,0:T(8,128)(2,1)S(1)}, u32[]{:S(2)}, u32[]{:S(2)}) %collective-permute-start.8) | collective-permute-done | bytes 131104 | tf_op jit(solution)/shard_map/while/body/eval_jaxpr/ppermute | solution.py:189
  94.1 1.3 collective-permute-start.11
  95.4 0.9 collective-permute-done.11.refs_3_
  104.9 3.4 %copy-done.1 = bf16[2048,2048]{1,0:T(8,128)(2,1)S(1)} copy-done((bf16[2048,2048]{1,0:T(8,128)(2,1)S(1)}, bf16[2048,2048]{1,0:T(8,128)(2,1)}, u32[]{:S(2)}) %copy-start.1) | copy-done | bytes 8388632 | tf_op jit(solution)/shard_map/while
  108.3 3.4 %copy-done.2 = bf16[2048,2048]{1,0:T(8,128)(2,1)S(1)} copy-done((bf16[2048,2048]{1,0:T(8,128)(2,1)S(1)}, bf16[2048,2048]{1,0:T(8,128)(2,1)}, u32[]{:S(2)}) %copy-start.2) | copy-done | bytes 8388632 | tf_op jit(solution)/shard_map/while
  113.0 3.3 %assemble.2.refs_1_ = bf16[2048,2048]{1,0:T(8,128)(2,1)S(1)} custom-call(s32[1]{0:T(128)S(6)} %sub.13._.refs_0_, s32[128]{0:T(128)} %bitcast.19, bf16[128,128,128]{2,1,0:T(8,128)(2,1)} %bitcast.16), custom_call_target="tpu_custom_call" | custom-call | tf_op jit(solution)/shard_map/assemble/pallas_call | solution.py:49
  120.7 1.3 collective-permute-start.32
  122.0 1.3 collective-permute-start.33
  123.3 59.0 %collective-permute-done.32.refs_3_ = bf16[64,1024]{1,0:T(8,128)(2,1)S(1)} collective-permute-done((bf16[64,1024]{1,0:T(8,128)(2,1)S(1)}, bf16[64,1024]{1,0:T(8,128)(2,1)S(1)}, u32[]{:S(2)}, u32[]{:S(2)}) %collective-permute-start.32) | collective-permute-done | bytes 131104 | tf_op jit(solution)/shard_map/ppermute | solution.py:189
  182.2 0.8 first.22.refs_2_
  184.8 1.3 collective-permute-start.35
  186.1 0.9 collective-permute-done.35.refs_3_
  187.0 0.7 pad_maximum_fusion
  (198 shorter events, 31.9 us)
Async XLA Ops:
  1.0 4.7 %collective-permute-start = (bf16[64,1024]{1,0:T(8,128)(2,1)S(1)}, bf16[64,1024]{1,0:T(8,128)(2,1)S(1)}, u32[]{:S(2)}, u32[]{:S(2)}) collective-permute-start(bf16[64,1024]{1,0:T(8,128)(2,1)S(1)} %get-tuple-element.198.refs_4_), channel_id=1, source_target_pairs={{0,1},{12,13},{27,28},{42,43},{57,58},{72,73},{87,88},{102,103},{1... | collective-permute-start | bytes 393224 | tf_op jit(solution)/shard_map/while/body/eval_jaxpr/ppermute | solution.py:189
  1.7 4.0 %collective-permute-start.1 = (bf16[64,1024]{1,0:T(8,128)(2,1)S(1)}, bf16[64,1024]{1,0:T(8,128)(2,1)S(1)}, u32[]{:S(2)}, u32[]{:S(2)}) collective-permute-start(bf16[64,1024]{1,0:T(8,128)(2,1)S(1)} %get-tuple-element.197.refs_4_), channel_id=1, source_target_pairs={{0,16},{12,28},{27,43},{42,58},{57,73},{72,88},{87,103},{102,118},... | collective-permute-start | bytes 393224 | tf_op jit(solution)/shard_map/while/body/eval_jaxpr/ppermute | solution.py:190
  5.8 1.4 collective-permute-start.2
  10.1 19.9 %collective-permute-start.8 = (bf16[64,1024]{1,0:T(8,128)(2,1)S(1)}, bf16[64,1024]{1,0:T(8,128)(2,1)S(1)}, u32[]{:S(2)}, u32[]{:S(2)}) collective-permute-start(bf16[64,1024]{1,0:T(8,128)(2,1)S(1)} %top.31.refs_4_), channel_id=1, source_target_pairs={{4,5},{19,20},{34,35},{46,47},{49,50},{61,62},{64,65},{76,77},{91,... | collective-permute-start | bytes 393224 | tf_op jit(solution)/shard_map/while/body/eval_jaxpr/ppermute | solution.py:189
  11.4 18.6 %collective-permute-start.9 = (bf16[64,1024]{1,0:T(8,128)(2,1)S(1)}, bf16[64,1024]{1,0:T(8,128)(2,1)S(1)}, u32[]{:S(2)}, u32[]{:S(2)}) collective-permute-start(bf16[64,1024]{1,0:T(8,128)(2,1)S(1)} %right.31.refs_4_), channel_id=1, source_target_pairs={{4,20},{19,35},{31,47},{34,50},{46,62},{49,65},{61,77},{64,80},{76... | collective-permute-start | bytes 393224 | tf_op jit(solution)/shard_map/while/body/eval_jaxpr/ppermute | solution.py:190
  30.0 2.0 %collective-permute-start.10 = (bf16[64,1024]{1,0:T(8,128)(2,1)S(1)}, bf16[64,1024]{1,0:T(8,128)(2,1)S(1)}, u32[]{:S(2)}, u32[]{:S(2)}) collective-permute-start(bf16[64,1024]{1,0:T(8,128)(2,1)S(1)} %top.32.refs_4_), channel_id=1, source_target_pairs={{5,6},{20,21},{35,36},{50,51},{62,63},{65,66},{77,78},{80,81},{92,... | collective-permute-start | bytes 393224 | tf_op jit(solution)/shard_map/while/body/eval_jaxpr/ppermute | solution.py:189
  30.7 2.3 %collective-permute-start.11 = (bf16[64,1024]{1,0:T(8,128)(2,1)S(1)}, bf16[64,1024]{1,0:T(8,128)(2,1)S(1)}, u32[]{:S(2)}, u32[]{:S(2)}) collective-permute-start(bf16[64,1024]{1,0:T(8,128)(2,1)S(1)} %right.32.refs_4_), channel_id=1, source_target_pairs={{5,21},{20,36},{35,51},{47,63},{50,66},{62,78},{65,81},{77,93},{80... | collective-permute-start | bytes 393224 | tf_op jit(solution)/shard_map/while/body/eval_jaxpr/ppermute | solution.py:190
  34.4 1.4 collective-permute-start.14
  35.8 1.4 collective-permute-start.16
  37.2 1.4 collective-permute-start.18
  38.7 1.4 collective-permute-start.20
  40.1 4.8 %collective-permute-start.22 = (bf16[64,1024]{1,0:T(8,128)(2,1)S(1)}, bf16[64,1024]{1,0:T(8,128)(2,1)S(1)}, u32[]{:S(2)}, u32[]{:S(2)}) collective-permute-start(bf16[64,1024]{1,0:T(8,128)(2,1)S(1)} %top.38.refs_4_), channel_id=1, source_target_pairs={{11,12},{26,27},{41,42},{56,57},{71,72},{86,87},{101,102},{116,117... | collective-permute-start | bytes 393224 | tf_op jit(solution)/shard_map/while/body/eval_jaxpr/ppermute | solution.py:189
  40.8 7.4 %collective-permute-start.23 = (bf16[64,1024]{1,0:T(8,128)(2,1)S(1)}, bf16[64,1024]{1,0:T(8,128)(2,1)S(1)}, u32[]{:S(2)}, u32[]{:S(2)}) collective-permute-start(bf16[64,1024]{1,0:T(8,128)(2,1)S(1)} %right.38.after.refs_4_), channel_id=1, source_target_pairs={{11,27},{26,42},{41,57},{56,72},{71,87},{86,102},{101,117},{116,13... | collective-permute-start | bytes 393224 | tf_op jit(solution)/shard_map/while/body/eval_jaxpr/ppermute | solution.py:190
  48.2 4.7 %collective-permute-start = (bf16[64,1024]{1,0:T(8,128)(2,1)S(1)}, bf16[64,1024]{1,0:T(8,128)(2,1)S(1)}, u32[]{:S(2)}, u32[]{:S(2)}) collective-permute-start(bf16[64,1024]{1,0:T(8,128)(2,1)S(1)} %get-tuple-element.198.refs_4_), channel_id=1, source_target_pairs={{0,1},{12,13},{27,28},{42,43},{57,58},{72,73},{87,88},{102,103},{1... | collective-permute-start | bytes 393224 | tf_op jit(solution)/shard_map/while/body/eval_jaxpr/ppermute | solution.py:189
  48.9 4.0 %collective-permute-start.1 = (bf16[64,1024]{1,0:T(8,128)(2,1)S(1)}, bf16[64,1024]{1,0:T(8,128)(2,1)S(1)}, u32[]{:S(2)}, u32[]{:S(2)}) collective-permute-start(bf16[64,1024]{1,0:T(8,128)(2,1)S(1)} %get-tuple-element.197.refs_4_), channel_id=1, source_target_pairs={{0,16},{12,28},{27,43},{42,58},{57,73},{72,88},{87,103},{102,118},... | collective-permute-start | bytes 393224 | tf_op jit(solution)/shard_map/while/body/eval_jaxpr/ppermute | solution.py:190
  53.0 1.4 collective-permute-start.2
  54.4 1.4 collective-permute-start.4
  55.8 1.4 collective-permute-start.6
  57.3 36.2 %collective-permute-start.8 = (bf16[64,1024]{1,0:T(8,128)(2,1)S(1)}, bf16[64,1024]{1,0:T(8,128)(2,1)S(1)}, u32[]{:S(2)}, u32[]{:S(2)}) collective-permute-start(bf16[64,1024]{1,0:T(8,128)(2,1)S(1)} %top.31.refs_4_), channel_id=1, source_target_pairs={{4,5},{19,20},{34,35},{46,47},{49,50},{61,62},{64,65},{76,77},{91,... | collective-permute-start | bytes 393224 | tf_op jit(solution)/shard_map/while/body/eval_jaxpr/ppermute | solution.py:189
  58.6 34.8 %collective-permute-start.9 = (bf16[64,1024]{1,0:T(8,128)(2,1)S(1)}, bf16[64,1024]{1,0:T(8,128)(2,1)S(1)}, u32[]{:S(2)}, u32[]{:S(2)}) collective-permute-start(bf16[64,1024]{1,0:T(8,128)(2,1)S(1)} %right.31.refs_4_), channel_id=1, source_target_pairs={{4,20},{19,35},{31,47},{34,50},{46,62},{49,65},{61,77},{64,80},{76... | collective-permute-start | bytes 393224 | tf_op jit(solution)/shard_map/while/body/eval_jaxpr/ppermute | solution.py:190
  93.4 2.0 %collective-permute-start.10 = (bf16[64,1024]{1,0:T(8,128)(2,1)S(1)}, bf16[64,1024]{1,0:T(8,128)(2,1)S(1)}, u32[]{:S(2)}, u32[]{:S(2)}) collective-permute-start(bf16[64,1024]{1,0:T(8,128)(2,1)S(1)} %top.32.refs_4_), channel_id=1, source_target_pairs={{5,6},{20,21},{35,36},{50,51},{62,63},{65,66},{77,78},{80,81},{92,... | collective-permute-start | bytes 393224 | tf_op jit(solution)/shard_map/while/body/eval_jaxpr/ppermute | solution.py:189
  94.1 2.3 %collective-permute-start.11 = (bf16[64,1024]{1,0:T(8,128)(2,1)S(1)}, bf16[64,1024]{1,0:T(8,128)(2,1)S(1)}, u32[]{:S(2)}, u32[]{:S(2)}) collective-permute-start(bf16[64,1024]{1,0:T(8,128)(2,1)S(1)} %right.32.refs_4_), channel_id=1, source_target_pairs={{5,21},{20,36},{35,51},{47,63},{50,66},{62,78},{65,81},{77,93},{80... | collective-permute-start | bytes 393224 | tf_op jit(solution)/shard_map/while/body/eval_jaxpr/ppermute | solution.py:190
  103.5 4.8 %collective-permute-start.22 = (bf16[64,1024]{1,0:T(8,128)(2,1)S(1)}, bf16[64,1024]{1,0:T(8,128)(2,1)S(1)}, u32[]{:S(2)}, u32[]{:S(2)}) collective-permute-start(bf16[64,1024]{1,0:T(8,128)(2,1)S(1)} %top.38.refs_4_), channel_id=1, source_target_pairs={{11,12},{26,27},{41,42},{56,57},{71,72},{86,87},{101,102},{116,117... | collective-permute-start | bytes 393224 | tf_op jit(solution)/shard_map/while/body/eval_jaxpr/ppermute | solution.py:189
  104.2 7.4 %collective-permute-start.23 = (bf16[64,1024]{1,0:T(8,128)(2,1)S(1)}, bf16[64,1024]{1,0:T(8,128)(2,1)S(1)}, u32[]{:S(2)}, u32[]{:S(2)}) collective-permute-start(bf16[64,1024]{1,0:T(8,128)(2,1)S(1)} %right.38.after.refs_4_), channel_id=1, source_target_pairs={{11,27},{26,42},{41,57},{56,72},{71,87},{86,102},{101,117},{116,13... | collective-permute-start | bytes 393224 | tf_op jit(solution)/shard_map/while/body/eval_jaxpr/ppermute | solution.py:190
  111.7 4.7 %collective-permute-start.24 = (bf16[64,1024]{1,0:T(8,128)(2,1)S(1)}, bf16[64,1024]{1,0:T(8,128)(2,1)S(1)}, u32[]{:S(2)}, u32[]{:S(2)}) collective-permute-start(bf16[64,1024]{1,0:T(8,128)(2,1)S(1)} %get-tuple-element.128.refs_4_), channel_id=1, source_target_pairs={{0,1},{12,13},{27,28},{42,43},{57,58},{72,73},{87,88},{102,103},{1... | collective-permute-start | bytes 393224 | tf_op jit(solution)/shard_map/ppermute | solution.py:189
  112.3 4.0 %collective-permute-start.25 = (bf16[64,1024]{1,0:T(8,128)(2,1)S(1)}, bf16[64,1024]{1,0:T(8,128)(2,1)S(1)}, u32[]{:S(2)}, u32[]{:S(2)}) collective-permute-start(bf16[64,1024]{1,0:T(8,128)(2,1)S(1)} %get-tuple-element.129.refs_4_), channel_id=1, source_target_pairs={{0,16},{12,28},{27,43},{42,58},{57,73},{72,88},{87,103},{102,118},... | collective-permute-start | bytes 393224 | tf_op jit(solution)/shard_map/ppermute | solution.py:190
  116.4 1.4 collective-permute-start.26
  117.8 1.4 collective-permute-start.28
  120.7 61.6 %collective-permute-start.32 = (bf16[64,1024]{1,0:T(8,128)(2,1)S(1)}, bf16[64,1024]{1,0:T(8,128)(2,1)S(1)}, u32[]{:S(2)}, u32[]{:S(2)}) collective-permute-start(bf16[64,1024]{1,0:T(8,128)(2,1)S(1)} %top.25.refs_4_), channel_id=1, source_target_pairs={{4,5},{19,20},{34,35},{46,47},{49,50},{61,62},{64,65},{76,77},{91,... | collective-permute-start | bytes 393224 | tf_op jit(solution)/shard_map/ppermute | solution.py:189
  122.0 61.1 %collective-permute-start.33 = (bf16[64,1024]{1,0:T(8,128)(2,1)S(1)}, bf16[64,1024]{1,0:T(8,128)(2,1)S(1)}, u32[]{:S(2)}, u32[]{:S(2)}) collective-permute-start(bf16[64,1024]{1,0:T(8,128)(2,1)S(1)} %right.25.refs_4_), channel_id=1, source_target_pairs={{4,20},{19,35},{31,47},{34,50},{46,62},{49,65},{61,77},{64,80},{76... | collective-permute-start | bytes 393224 | tf_op jit(solution)/shard_map/ppermute | solution.py:190
  183.6 2.5 %collective-permute-start.34 = (bf16[64,1024]{1,0:T(8,128)(2,1)S(1)}, bf16[64,1024]{1,0:T(8,128)(2,1)S(1)}, u32[]{:S(2)}, u32[]{:S(2)}) collective-permute-start(bf16[64,1024]{1,0:T(8,128)(2,1)S(1)} %top.26.refs_4_), channel_id=1, source_target_pairs={{5,6},{20,21},{35,36},{50,51},{62,63},{65,66},{77,78},{80,81},{92,... | collective-permute-start | bytes 393224 | tf_op jit(solution)/shard_map/ppermute | solution.py:189
  184.8 2.3 %collective-permute-start.35 = (bf16[64,1024]{1,0:T(8,128)(2,1)S(1)}, bf16[64,1024]{1,0:T(8,128)(2,1)S(1)}, u32[]{:S(2)}, u32[]{:S(2)}) collective-permute-start(bf16[64,1024]{1,0:T(8,128)(2,1)S(1)} %right.26.refs_4_), channel_id=1, source_target_pairs={{5,21},{20,36},{35,51},{47,63},{50,66},{62,78},{65,81},{77,93},{80... | collective-permute-start | bytes 393224 | tf_op jit(solution)/shard_map/ppermute | solution.py:190
  (34 other events, 125.6 us)
